TPU v7x, 128 devices: a whole 4x4x4 slice. The times are simulated.
128 devices in a mesh: shell: 64 (over y, x, z), sky: 2 (over core).
Axes of the slice: x: 4, y: 4, z: 4, core: 2. Of those that a mesh axis runs over, the one named last changes fastest.
Arguments:
- excitation: float32 [2048, 65536], P('shell', 'sky'), may hold values from -1.8 to 1.8
- star_shell: int32 [128, 128, 128], P(('shell', 'sky')), may hold values from 0 to 31
- star_pixel: int32 [128, 128, 128], P(('shell', 'sky')), may hold values from 0 to 32767
- star_fraction: float32 [128, 128, 128], P(('shell', 'sky')), may hold values from 0 to 1
- star_count: int32 [128, 128], P(('shell', 'sky')), may hold values from 0 to 128, as said below
- observed: float32 [128, 128, 128], P(None, ('shell', 'sky')), may hold values from 0 to 1
- inverse_error: float32 [128, 128, 128], P(None, ('shell', 'sky')), may hold values from 1 to 8
Outputs:
- extinction: float32 [2048, 65536], P('shell', 'sky')
- sensitivity: float32 [2048, 65536], P('shell', 'sky')
- residual: float32 [128, 128, 128], P(None, ('shell', 'sky'))
Inputs may be any that keep to these rules, and one draw needn't show every extreme that they name: `star_count`: live slots from holder h to owner o. In every draw some owner gets 128 live slots from every holder; holders' loads differ.
All inputs are finite; a program needn't handle non-finite values.
Results may differ from a plain program's by a relative error of at most 0.00018.
Values sent between devices are 32-bit elements; how exact they have to be, the bound alone decides.
No kernel may reach another device: no remote copies, remote signals or barrier semaphores. Data moves between devices by JAX's collectives and lax.ppermute only.
A program may use at most 128 MiB of HBM per device.

v0:
```python
import jax
import jax.numpy as jnp
from jax import lax
from jax.sharding import PartitionSpec as P

PASSES = 4


depth_span = 2.0


def padded_2(shard, sides, width):
    for axis, dim in sides:
        size, length = (lax.axis_size(axis), shard.shape[dim])
        up = [(i, (i + 1) % size) for i in range(size - 1)]
        down = [(j, i) for i, j in up]
        last = lax.slice_in_dim(shard, length - width, length, axis=dim)
        leading = lax.slice_in_dim(shard, 0, width, axis=dim)
        before = lax.ppermute(last, axis, up)
        after = lax.ppermute(leading, axis, down)
        shard = jnp.concatenate([before, shard, after], axis=dim)
    return shard


def body(excitation, star_shell, star_pixel, star_fraction, star_count, observed, inverse_error):
    shell_rows = excitation.shape[0]
    pixel_cols = excitation.shape[1]
    shell_devices = lax.axis_size("shell")
    shells_all = shell_rows * shell_devices
    my_block = lax.axis_index("shell")
    thickness = depth_span / shells_all
    logdens = excitation
    for sweep in range(PASSES):
        padded = padded_2(logdens, (("shell", 0),), 1)
        logdens = 0.3 * (padded[:-2] + padded[2:]) + 0.35 * logdens + excitation
    density = jnp.exp(logdens)
    row_ids = jnp.arange(shell_rows, dtype=jnp.int32)
    lower_ones = (row_ids[:, None] >= row_ids[None, :]).astype(jnp.float32)
    upper_ones = (row_ids[:, None] <= row_ids[None, :]).astype(jnp.float32)
    local_prefix = jnp.dot(
        lower_ones,
        density * thickness,
        precision=lax.Precision.HIGHEST,
        preferred_element_type=jnp.float32,
    )
    block_ids = jnp.arange(shell_devices, dtype=jnp.int32)
    gathered = lax.all_gather(local_prefix[-1:], "shell", axis=0, tiled=True)
    below_mask = (block_ids < my_block).astype(jnp.float32)
    offset = jnp.dot(
        below_mask, gathered, precision=lax.Precision.HIGHEST, preferred_element_type=jnp.float32
    )
    extinction = local_prefix + offset[None, :]
    slot_shape = star_shell.shape
    cell_count = shell_rows * pixel_cols
    flat_cell = (star_shell * pixel_cols + star_pixel).reshape(-1)
    ext_at = jnp.take(extinction.reshape(-1), flat_cell).reshape(slot_shape)
    dens_at = jnp.take(density.reshape(-1), flat_cell).reshape(slot_shape)
    slot_alive = (
        jnp.arange(slot_shape[2], dtype=jnp.int32)[None, None, :] < star_count[:, :, None]
    ).astype(jnp.int32)
    near_share = 1.0 - star_fraction
    looked = ext_at - near_share * thickness * dens_at
    column = jnp.where(slot_alive > 0, looked, 0.0)
    owner_column, owner_alive = (
        lax.all_to_all(column, ("shell", "sky"), split_axis=1, concat_axis=0, tiled=True),
        lax.all_to_all(slot_alive, ("shell", "sky"), split_axis=1, concat_axis=0, tiled=True),
    )
    transmit = jnp.exp(-owner_column)
    residual = jnp.where(owner_alive > 0, (observed - (1.0 - transmit)) * inverse_error, 0.0)
    pull_back = -residual * inverse_error * transmit
    returned = lax.all_to_all(pull_back, ("shell", "sky"), split_axis=0, concat_axis=1, tiled=True)
    both_index = jnp.concatenate((flat_cell, flat_cell + cell_count), 0)
    both_values = jnp.concatenate((returned.reshape(-1), (near_share * returned).reshape(-1)), 0)
    accumulated = (
        jnp.zeros((2 * cell_count,), jnp.float32)
        .at[both_index]
        .add(both_values)
        .reshape(2, shell_rows, pixel_cols)
    )
    impulse = accumulated[0]
    nearby = accumulated[1]
    local_suffix = jnp.dot(
        upper_ones, impulse, precision=lax.Precision.HIGHEST, preferred_element_type=jnp.float32
    )
    gathered_tails = lax.all_gather(local_suffix[:1], "shell", axis=0, tiled=True)
    above_mask = (block_ids > my_block).astype(jnp.float32)
    tail_offset = jnp.dot(
        above_mask,
        gathered_tails,
        precision=lax.Precision.HIGHEST,
        preferred_element_type=jnp.float32,
    )
    sensitivity = density * (local_suffix + tail_offset[None, :] - nearby)
    return (extinction, sensitivity, residual)


def solution(mesh):
    placed = (
        P("shell", "sky"),
        P(("shell", "sky"), None, None),
        P(("shell", "sky"), None, None),
        P(("shell", "sky"), None, None),
        P(("shell", "sky"), None),
        P(None, ("shell", "sky"), None),
        P(None, ("shell", "sky"), None),
    )
    return jax.shard_map(
        body,
        mesh=mesh,
        in_specs=placed,
        out_specs=(P("shell", "sky"), P("shell", "sky"), P(None, ("shell", "sky"), None)),
        check_vma=False,
    )
```

profile of v0, /device:TPU:1, one launch (start us, length us, event | category | flops | bytes accessed | tf_op | source)
XLA Modules:
  0.0 849.3 jit_solution(15086881055013536109)
XLA Ops:
  8.9 4.4 collective-permute-start
  15.5 4.5 collective-permute-done.1
  19.9 5.8 fusion.22
  25.9 2.9 collective-permute-start.2
  30.7 3.8 collective-permute-done.3
  36.3 4.4 collective-permute-start.4
  42.6 3.8 collective-permute-done.5
  48.1 4.0 collective-permute-start.6
  54.1 3.8 collective-permute-done.7
  57.9 1.8 fusion.10
  59.8 2.3 fusion.25
  62.1 2.0 copy-done.3
  65.6 24.3 %all-to-all-start = ((s32[1,128,128]{2,0,1:T(1,128)}), s32[1,128,128]{2,0,1:T(1,128)S(1)}, u32[]{:S(2)}, u32[]{:S(2)}) async-start(s32[1,128,128]{2,0,1:T(1,128)} %bitcast.8), calls=%async_computation | async-start | bytes 131072 | tf_op jit(solution)/shard_map/all_to_all | solution.py:66
  90.0 5.0 copy.47
  95.0 208.0 %gather_fusion.1 = f32[16384]{0:T(1024)S(1)} fusion(f32[1048576]{0:T(1024)} %bitcast.76, s32[16384]{0:T(1024)S(1)} %get-tuple-element.15), kind=kCustom, calls=%fused_computation.1.clone | custom fusion | bytes 196608 | tf_op jit(solution)/shard_map/jit(_take)/gather | solution.py:57
  303.1 10.6 %fusion.3 = f32[1,32768]{1,0:T(1,128)S(1)} fusion(f32[64,1,32768]{2,1,0:T(1,128)} %all-gather.5.cloned.1.call-done, s32[]{:T(128)S(6)} %axis_index.15), kind=kOutput, calls=%fused_computation.6 | convolution fusion | flops 25165888 | bytes 8519684 | tf_op jit(solution)/shard_map/dot_general | solution.py:49
  313.9 2.8 copy.46
  316.7 206.7 %gather_fusion = f32[16384]{0:T(1024)S(1)} fusion(f32[1048576]{0:T(1024)} %bitcast.75, s32[16384]{0:T(1024)S(1)} %get-tuple-element.15), kind=kCustom, calls=%fused_computation.clone | custom fusion | bytes 196608 | tf_op jit(solution)/shard_map/jit(_take)/gather | solution.py:56
  524.2 9.5 %all-to-all-start.1 = ((f32[1,128,128]{2,0,1:T(1,128)}), f32[1,128,128]{2,0,1:T(1,128)S(1)}, u32[]{:S(2)}, u32[]{:S(2)}) async-start(f32[1,128,128]{2,0,1:T(1,128)} %bitcast.14), calls=%async_computation.1 | async-start | bytes 131072 | tf_op jit(solution)/shard_map/all_to_all | solution.py:65
  533.7 9.3 %all-to-all-done.1 = f32[1,128,128]{2,0,1:T(1,128)S(1)} async-done(((f32[1,128,128]{2,0,1:T(1,128)}), f32[1,128,128]{2,0,1:T(1,128)S(1)}, u32[]{:S(2)}, u32[]{:S(2)}) %all-to-all-start.1) | async-done | bytes 65568 | tf_op jit(solution)/shard_map/all_to_all | solution.py:65
  543.8 4.6 all-to-all-start.2
  548.6 9.3 %all-to-all-done.2 = f32[128,1,128]{2,1,0:T(1,128)S(1)} async-done(((f32[128,1,128]{2,1,0:T(1,128)}), f32[128,1,128]{2,1,0:T(1,128)S(1)}, u32[]{:S(2)}, u32[]{:S(2)}) %all-to-all-start.2) | async-done | bytes 65568 | tf_op jit(solution)/shard_map/all_to_all | solution.py:71
  557.9 174.8 %scatter_custom_fusion = f32[2097152]{0:T(1024)} fusion(s32[32768]{0:T(1024)S(1)} %bitcast.87, f32[32768]{0:T(1024)S(1)} %pad_maximum_fusion.8, f32[]{:T(128)} %constant.4.clone.1), kind=kCustom, calls=%fused_computation.35 | custom fusion | flops 32768 | bytes 8388612 | tf_op jit(solution)/shard_map/scatter-add | solution.py:77
  732.7 7.3 fusion.46
  740.0 5.0 slice.108
  744.9 4.4 fusion.35
  749.4 2.0 copy-done.5
  752.1 4.5 broadcast_add_fusion
  756.6 5.0 slice.111
  761.5 65.2 %all-gather.7.cloned.1.call-done = f32[64,1,32768]{2,1,0:T(1,128)} async-done(((f32[1,1,32768]{2,1,0:T(1,128)}), f32[64,1,32768]{2,1,0:T(1,128)}) %all-gather.7.cloned.1.call-update) | async-done | bytes 8388624 | tf_op jit(solution)/shard_map/all_gather | solution.py:85
  826.8 10.6 %fusion = f32[1,32768]{1,0:T(1,128)S(1)} fusion(f32[64,1,32768]{2,1,0:T(1,128)} %all-gather.7.cloned.1.call-done, s32[]{:T(128)S(6)} %axis_index.15), kind=kOutput, calls=%fused_computation.3 | convolution fusion | flops 25165888 | bytes 8519684 | tf_op jit(solution)/shard_map/dot_general | solution.py:87
  837.3 5.1 subtract_multiply_fusion
  (55 shorter events, 17.5 us)
Async XLA Ops:
  7.2 295.9 %all-gather.5.cloned.1.call-start = ((), (), s32[]{:S(2)}) async-start(), calls=%async_computation.3 | async-start | bytes 8519680 | tf_op jit(solution)/shard_map/all_gather | solution.py:47
  8.9 6.5 collective-permute-start
  13.3 21.2 %copy-start = (f32[32,32768]{1,0:T(8,128)S(1)}, f32[32,32768]{1,0:T(8,128)}, u32[]{:S(2)}) copy-start(f32[32,32768]{1,0:T(8,128)} %param.9) | copy-start | bytes 12582916
  13.3 6.6 collective-permute-start.1
  25.9 4.8 collective-permute-start.2
  28.8 5.7 collective-permute-start.3
  36.3 6.3 collective-permute-start.4
  40.7 5.7 collective-permute-start.5
  48.1 6.0 collective-permute-start.6
  52.2 5.7 collective-permute-start.7
  59.7 2.3 copy-start.1
  59.7 5.2 copy-start.12
  59.8 30.2 %copy-start.8 = (s32[1,128,128]{2,1,0:T(8,128)S(1)}, s32[1,128,128]{2,1,0:T(8,128)}, u32[]{:S(2)}) copy-start(s32[1,128,128]{2,1,0:T(8,128)} %param.11) | copy-start | bytes 196612
  59.8 30.2 %copy-start.9 = (s32[1,128,128]{2,1,0:T(8,128)S(1)}, s32[1,128,128]{2,1,0:T(8,128)}, u32[]{:S(2)}) copy-start(s32[1,128,128]{2,1,0:T(8,128)} %param.10) | copy-start | bytes 196612
  62.1 2.0 copy-start.3
  65.6 458.6 %all-to-all-start = ((s32[1,128,128]{2,0,1:T(1,128)}), s32[1,128,128]{2,0,1:T(1,128)S(1)}, u32[]{:S(2)}, u32[]{:S(2)}) async-start(s32[1,128,128]{2,0,1:T(1,128)} %bitcast.8), calls=%async_computation | async-start | bytes 131072 | tf_op jit(solution)/shard_map/all_to_all | solution.py:66
  303.0 10.6 %copy-start.4 = (f32[32,32768]{1,0:T(8,128)S(1)}, f32[32,32768]{1,0:T(8,128)}, u32[]{:S(2)}) copy-start(f32[32,32768]{1,0:T(8,128)} %copy-done.3) | copy-start | bytes 12582916
  316.7 206.8 %copy-start.7 = (f32[1,128,128]{2,1,0:T(8,128)S(1)}, f32[1,128,128]{2,1,0:T(8,128)}, u32[]{:S(2)}) copy-start(f32[1,128,128]{2,1,0:T(8,128)} %param.12) | copy-start | bytes 196612
  316.7 226.4 %copy-start.10 = (f32[128,1,128]{2,1,0:T(1,128)S(1)}, f32[128,1,128]{2,1,0:T(1,128)}, u32[]{:S(2)}) copy-start(f32[128,1,128]{2,1,0:T(1,128)} %param.15) | copy-start | bytes 196612
  316.7 226.4 %copy-start.11 = (f32[128,1,128]{2,1,0:T(1,128)S(1)}, f32[128,1,128]{2,1,0:T(1,128)}, u32[]{:S(2)}) copy-start(f32[128,1,128]{2,1,0:T(1,128)} %param.14) | copy-start | bytes 196612
  524.2 18.9 %all-to-all-start.1 = ((f32[1,128,128]{2,0,1:T(1,128)}), f32[1,128,128]{2,0,1:T(1,128)S(1)}, u32[]{:S(2)}, u32[]{:S(2)}) async-start(f32[1,128,128]{2,0,1:T(1,128)} %bitcast.14), calls=%async_computation.1 | async-start | bytes 131072 | tf_op jit(solution)/shard_map/all_to_all | solution.py:65
  543.8 14.1 %all-to-all-start.2 = ((f32[128,1,128]{2,1,0:T(1,128)}), f32[128,1,128]{2,1,0:T(1,128)S(1)}, u32[]{:S(2)}, u32[]{:S(2)}) async-start(f32[128,1,128]{2,1,0:T(1,128)} %bitcast.19), calls=%async_computation.2 | async-start | bytes 131072 | tf_op jit(solution)/shard_map/all_to_all | solution.py:71
  548.4 278.4 %all-gather.7.cloned.1.call-start = ((), (), s32[]{:S(2)}) async-start(), calls=%async_computation.4 | async-start | bytes 8519680 | tf_op jit(solution)/shard_map/all_gather | solution.py:85
  749.4 2.0 copy-start.5
  826.8 10.6 %copy-start.2 = (f32[32,32768]{1,0:T(8,128)S(1)}, f32[32,32768]{1,0:T(8,128)}, u32[]{:S(2)}) copy-start(f32[32,32768]{1,0:T(8,128)} %copy-done.1) | copy-start | bytes 12582916
  826.8 10.6 %copy-start.6 = (f32[32,32768]{1,0:T(8,128)S(1)}, f32[32,32768]{1,0:T(8,128)}, u32[]{:S(2)}) copy-start(f32[32,32768]{1,0:T(8,128)} %copy-done.5) | copy-start | bytes 12582916
Sparse Core Ops, SparseCore 0:
  65.0 94.2 all-gather.4
  752.2 74.5 all-gather.6
where the time goes:
time: 864 us; the launch traced here: 849 us
  local copies, waits for them, and re-layouts  447 us (52%)
  other arithmetic  198 us (23%)
  waiting for transfers between devices  102 us (12%)
  starting transfers between devices  59.6 us (7%)
  matrix products  27.9 us (3%)
  between operations  14.4 us (2%)
    gather x1, local copies, waits for them, and re-layouts, body(): dens_at = jnp.take(density.reshape(-1), flat_cell).reshape(slot_shape)  208 us
    gather x1, local copies, waits for them, and re-layouts, body(): ext_at = jnp.take(extinction.reshape(-1), flat_cell).reshape(slot_shape)  207 us
    scatter-add x1, other arithmetic, body(): accumulated = jnp.zeros((2 * cell_count,), jnp.float32).at[both_index].ad...  175 us
    all_gather x1, waiting for transfers between devices, body(): lax.all_gather(local_suffix[:1], 'shell', axis=0, tiled=True)  65.2 us
    all_to_all x1, starting transfers between devices, body(): lax.all_to_all(slot_alive, ('shell', 'sky'), split_axis=1, concat_axis=0,...  24.3 us
  transfers between devices with their start and end apart: 13, of which 11 were waited for; matrix products, arithmetic and copies ran while one was open for 52% of the time, Pallas kernels for 0%

commit v1 on v0

v1 whole, which is shorter than its diff:
```python
import jax
import jax.numpy as jnp
from jax import lax
from jax.experimental import pallas as pl
from jax.experimental.pallas import tpu as pltpu
from jax.sharding import PartitionSpec as P

PASSES = 4
LANES = 128
SUB = 8
SPARE = 8
ACCS = 4
BOTH = ("shell", "sky")


depth_span = 2.0


def cost(micros, nbytes):
    return pl.CostEstimate(flops=int(micros * 2e8), bytes_accessed=int(nbytes), transcendentals=0)


def density_kernel(shells, thickness, edge_ref, exc_ref, up_ref, down_ref, dens_ref, tab_ref, sum_ref):
    tall = shells + 1
    low_mask = edge_ref[0]
    high_mask = edge_ref[1]

    def group(g):
        exc = {}

        def load(r):
            if r < 0:
                return up_ref[pl.ds(g * SUB * PASSES + PASSES + r, SUB, stride=PASSES), :]
            if r >= shells:
                return down_ref[pl.ds(g * SUB * PASSES + r - shells, SUB, stride=PASSES), :]
            return exc_ref.at[r // SUB][pl.ds(g * SUB * SUB + r % SUB, SUB, stride=SUB), :]

        level = [dict() for _ in range(PASSES + 1)]
        tab_ref[pl.ds(g * SUB * tall, SUB, stride=tall), :] = jnp.zeros((SUB, LANES), jnp.float32)
        total = None
        for t in range(-PASSES, shells + PASSES):
            exc[t] = load(t)
            level[0][t] = exc[t]
            for k in range(1, PASSES + 1):
                r = t - k
                reach = PASSES - k
                if r < -reach or r >= shells + reach:
                    continue
                below = level[k - 1]
                value = 0.3 * (below[r - 1] + below[r + 1]) + 0.35 * below[r] + exc[r]
                if r < 0:
                    value = value * low_mask
                if r >= shells:
                    value = value * high_mask
                level[k][r] = value
            r = t - PASSES
            if r >= 0:
                dens = jnp.exp(level[PASSES][r])
                dens_ref[pl.ds((g * shells + r) * SUB, SUB), :] = dens
                step = dens * thickness
                total = step if total is None else total + step
                tab_ref[pl.ds(g * SUB * tall + 1 + r, SUB, stride=tall), :] = total
        sum_ref[pl.ds(g * SUB, SUB), :] = total

    for g in range(sum_ref.shape[0] // SUB):
        group(g)


def density_call(exc, up, down, edge, shells, groups, thickness):
    per = 32
    tall = shells + 1
    return pl.pallas_call(
        lambda *refs: density_kernel(shells, thickness, *refs),
        grid=(groups // per,),
        in_specs=[
            pl.BlockSpec(memory_space=pltpu.SMEM),
            pl.BlockSpec((shells // SUB, per * SUB, LANES), lambda i: (0, i, 0)),
            pl.BlockSpec((per * PASSES, LANES), lambda i: (i, 0)),
            pl.BlockSpec((per * PASSES, LANES), lambda i: (i, 0)),
        ],
        out_specs=[
            pl.BlockSpec((per * shells, LANES), lambda i: (i, 0)),
            pl.BlockSpec((per * tall, LANES), lambda i: (i, 0)),
            pl.BlockSpec((per, LANES), lambda i: (i, 0)),
        ],
        out_shape=[
            jax.ShapeDtypeStruct((groups * shells, LANES), jnp.float32),
            jax.ShapeDtypeStruct((groups * tall + SPARE, LANES), jnp.float32),
            jax.ShapeDtypeStruct((groups, LANES), jnp.float32),
        ],
        cost_estimate=cost(8, 12 << 20),
        name="density",
    )(edge, exc, up, down)


def lookup_kernel(first, idx_ref, tab_ref, frac_ref, out_ref):
    lane = lax.broadcasted_iota(jnp.int32, (SUB, LANES), 1)

    def body(o, carry):
        acc = [jnp.zeros((SUB, LANES), jnp.float32) for _ in range(4)]
        for c in range(LANES):
            packed = idx_ref[o + first, c]
            row = lax.shift_right_logical(packed, 7)
            value = pltpu.roll(tab_ref[pl.ds(row, SUB), :], packed & 127, 1)
            acc[c % 4] = jnp.where(lane == c, value, acc[c % 4])
        got = (acc[0] + acc[1]) + (acc[2] + acc[3])
        inner, outer = got[0:1], got[1:2]
        out_ref[pl.ds(o, 1), :] = inner + frac_ref[pl.ds(o + first, 1), :] * (outer - inner)
        return carry

    lax.fori_loop(0, out_ref.shape[0], body, 0)


def lookup_call(idx, tab, frac, first, count):
    return pl.pallas_call(
        lambda *refs: lookup_kernel(first, *refs),
        out_shape=jax.ShapeDtypeStruct((count, LANES), jnp.float32),
        in_specs=[
            pl.BlockSpec(memory_space=pltpu.SMEM),
            pl.BlockSpec(memory_space=pltpu.VMEM),
            pl.BlockSpec(memory_space=pltpu.VMEM),
        ],
        out_specs=pl.BlockSpec(memory_space=pltpu.VMEM),
        cost_estimate=cost(17, 5 << 20),
        name="lookup",
    )(idx, tab, frac)


def scan_kernel(reverse, in_ref, out_ref):
    n = in_ref.shape[0]
    order = range(n - 1, -1, -1) if reverse else range(n)
    total = jnp.zeros(in_ref.shape[1:], jnp.float32)
    for i in order:
        out_ref[i] = total
        total = total + in_ref[i]


def scan_call(parts, reverse):
    return pl.pallas_call(
        lambda *refs: scan_kernel(reverse, *refs),
        out_shape=jax.ShapeDtypeStruct(parts.shape, jnp.float32),
        cost_estimate=cost(1, 1 << 18),
        name="scan",
    )(parts)


def exclusive_sums(block, reverse):
    devices = lax.axis_size("shell")
    parts = block.reshape(devices, block.shape[0] // devices, LANES)
    parts = lax.all_to_all(parts, "shell", split_axis=0, concat_axis=0, tiled=True)
    parts = scan_call(parts, reverse)
    parts = lax.all_to_all(parts, "shell", split_axis=0, concat_axis=0, tiled=True)
    return parts.reshape(block.shape)


def halves(x):
    high = x.astype(jnp.bfloat16)
    return high, (x - high.astype(jnp.float32)).astype(jnp.bfloat16)


def star_kernel(pix_ref, off_ref, col_a_ref, col_b_ref, frac_ref, alive_ref, obs_ref, inv_ref,
                res_ref, here_ref, inner_ref, tail_ref, acc_ref):
    groups = off_ref.shape[0]
    rows = SUB
    offt = jnp.transpose(off_ref[...])
    offt = jnp.concatenate(halves(offt), axis=0)
    group_id = lax.broadcasted_iota(jnp.int32, (groups, LANES), 0)
    lane_id = lax.broadcasted_iota(jnp.int32, (LANES, LANES), 0)
    acc_ref[...] = jnp.zeros_like(acc_ref)

    def body(b, col_ref, shift):
        at = pl.ds(pl.multiple_of(b * rows, rows), rows)
        local = pl.ds(pl.multiple_of((b - shift) * rows, rows), rows)
        pix = pix_ref[at, :]
        high = lax.shift_right_logical(pix, 7)
        low = pix & 127
        pick = jnp.concatenate(
            [jnp.where(group_id == high[j:j + 1, :], 1.0, 0.0).astype(jnp.bfloat16) for j in range(rows)], axis=1)
        found = jnp.dot(offt, pick, preferred_element_type=jnp.float32)
        lanes = [lane_id == low[j:j + 1, :] for j in range(rows)]
        off_at = []
        for j in range(rows):
            part = found[:, j * LANES:(j + 1) * LANES]
            part = jnp.where(lanes[j], part[:LANES] + part[LANES:], 0.0)
            off_at.append(jnp.sum(part, axis=0, keepdims=True))
        column = col_ref[local, :] + jnp.concatenate(off_at, axis=0)
        transmit = jnp.exp(-column)
        inv = inv_ref[at, :]
        residual = jnp.where(alive_ref[at, :] > 0.0, (obs_ref[at, :] - (1.0 - transmit)) * inv, 0.0)
        pull = -residual * inv * transmit
        inner = (1.0 - frac_ref[at, :]) * pull
        res_ref[at, :] = residual
        here_ref[at, :] = pull - inner
        inner_ref[at, :] = inner
        spread = []
        for j in range(rows):
            spread.append(jnp.concatenate(halves(jnp.where(lanes[j], pull[j:j + 1, :], 0.0)), axis=0))
        spread = jnp.concatenate(spread, axis=1)
        acc_ref[...] += lax.dot_general(
            pick, spread, (((1,), (1,)), ((), ())), preferred_element_type=jnp.float32)

    half = col_a_ref.shape[0] // rows
    full = pix_ref.shape[0] // rows

    @pl.loop(0, half)
    def _(b):
        body(b, col_a_ref, 0)

    @pl.loop(half, full)
    def _(b):
        body(b, col_b_ref, half)

    tail_ref[...] = acc_ref[:, :LANES] + acc_ref[:, LANES:]


def star_call(pix, off, col_a, col_b, frac, alive, obs, inv):
    slots = jax.ShapeDtypeStruct(pix.shape, jnp.float32)
    return pl.pallas_call(
        star_kernel,
        out_shape=[slots, slots, slots, jax.ShapeDtypeStruct(off.shape, jnp.float32)],
        scratch_shapes=[pltpu.VMEM((off.shape[0], 2 * LANES), jnp.float32)],
        cost_estimate=cost(8, 1 << 20),
        name="star",
    )(pix, off, col_a, col_b, frac, alive, obs, inv)


def spread_kernel(first, count, start, idx_ref, here_ref, inner_ref, *refs):
    if start:
        start_ref, out_ref = refs[0], refs[1]
        accs = refs[2:]
    else:
        out_ref = refs[0]
        accs = refs[1:]
    total_rows = out_ref.shape[0]
    chunk = 64
    chunks = total_rows // chunk
    rest = total_rows - chunks * chunk

    def over(fn):
        def step(i, carry):
            fn(pl.ds(pl.multiple_of(i * chunk, chunk), chunk), chunk)
            return carry
        lax.fori_loop(0, chunks, step, 0)
        if rest:
            fn(pl.ds(chunks * chunk, rest), rest)

    def clear(rows, n):
        for k, acc in enumerate(accs):
            acc[rows, :] = start_ref[rows, :] if start and k == 0 else jnp.zeros((n, LANES), jnp.float32)

    over(clear)
    lane = lax.broadcasted_iota(jnp.int32, (SUB, LANES), 1)
    sub = lax.broadcasted_iota(jnp.int32, (SUB, LANES), 0)
    lane_a = jnp.where(sub == 0, lane, -1)
    lane_b = jnp.where(sub == 1, lane, -1)

    def body(o, carry):
        for c in range(LANES):
            packed = idx_ref[o, c]
            row = lax.shift_right_logical(packed, 7)
            low = packed & 127
            value = jnp.where(lane_a == low, inner_ref[o, c], jnp.where(lane_b == low, here_ref[o, c], 0.0))
            acc = accs[c % ACCS]
            acc[pl.ds(row, SUB), :] = acc[pl.ds(row, SUB), :] + value
        return carry

    lax.fori_loop(first, first + count, body, 0)

    def gather(rows, n):
        total = accs[0][rows, :]
        for acc in accs[1:]:
            total = total + acc[rows, :]
        out_ref[rows, :] = total

    over(gather)


def spread_call(idx, here, inner, rows, first, count, start=None):
    shape = (rows, LANES)
    extra = () if start is None else (start,)
    return pl.pallas_call(
        lambda *refs: spread_kernel(first, count, start is not None, *refs),
        out_shape=jax.ShapeDtypeStruct(shape, jnp.float32),
        in_specs=[pl.BlockSpec(memory_space=pltpu.SMEM)] * 3
        + [pl.BlockSpec(memory_space=pltpu.VMEM)] * len(extra),
        out_specs=pl.BlockSpec(memory_space=pltpu.VMEM),
        scratch_shapes=[pltpu.VMEM(shape, jnp.float32)] * ACCS,
        cost_estimate=cost(20, 5 << 20),
        name="spread",
    )(idx, here, inner, *extra)


def extinction_kernel(shells, tab_ref, off_ref, out_ref):
    tall = shells + 1
    for g in range(off_ref.shape[0] // SUB):
        off = off_ref[pl.ds(g * SUB, SUB), :]
        for r in range(shells):
            value = tab_ref[pl.ds(g * SUB * tall + 1 + r, SUB, stride=tall), :] + off
            out_ref.at[r // SUB][pl.ds(g * SUB * SUB + r % SUB, SUB, stride=SUB), :] = value


def extinction_call(tab, off, shells):
    groups = off.shape[0]
    per = 32
    return pl.pallas_call(
        lambda *refs: extinction_kernel(shells, *refs),
        grid=(groups // per,),
        in_specs=[
            pl.BlockSpec((per * (shells + 1), LANES), lambda i: (i, 0)),
            pl.BlockSpec((per, LANES), lambda i: (i, 0)),
        ],
        out_specs=pl.BlockSpec((shells // SUB, per * SUB, LANES), lambda i: (0, i, 0)),
        out_shape=jax.ShapeDtypeStruct((shells // SUB, groups * SUB, LANES), jnp.float32),
        cost_estimate=cost(4, 8 << 20),
        name="extinction",
    )(tab, off)


def sensitivity_kernel(shells, dens_ref, drop_ref, off_ref, out_ref):
    tall = shells + 1
    for g in range(off_ref.shape[0] // SUB):
        total = off_ref[pl.ds(g * SUB, SUB), :]
        for r in range(shells - 1, -1, -1):
            total = total + drop_ref[pl.ds(g * SUB * tall + 1 + r, SUB, stride=tall), :]
            out_ref.at[r // SUB][pl.ds(g * SUB * SUB + r % SUB, SUB, stride=SUB), :] = (
                dens_ref[pl.ds((g * shells + r) * SUB, SUB), :] * total)


def sensitivity_call(dens, drop, off, shells):
    groups = off.shape[0]
    per = 32
    return pl.pallas_call(
        lambda *refs: sensitivity_kernel(shells, *refs),
        grid=(groups // per,),
        in_specs=[
            pl.BlockSpec((per * shells, LANES), lambda i: (i, 0)),
            pl.BlockSpec((per * (shells + 1), LANES), lambda i: (i, 0)),
            pl.BlockSpec((per, LANES), lambda i: (i, 0)),
        ],
        out_specs=pl.BlockSpec((shells // SUB, per * SUB, LANES), lambda i: (0, i, 0)),
        out_shape=jax.ShapeDtypeStruct((shells // SUB, groups * SUB, LANES), jnp.float32),
        cost_estimate=cost(5, 12 << 20),
        name="sensitivity",
    )(dens, drop, off)


def to_tiles(x):
    shells, pixels = x.shape
    groups = pixels // LANES
    x = x.reshape(shells // SUB, SUB, groups, LANES).transpose(0, 2, 1, 3)
    return x.reshape(shells // SUB, groups * SUB, LANES)


def from_tiles(x):
    bands, rows, lanes = x.shape
    groups = rows // SUB
    x = x.reshape(bands, groups, SUB, lanes).transpose(0, 2, 1, 3)
    return x.reshape(bands * SUB, groups * lanes)


def edge_rows(x, rows):
    count, pixels = rows.stop - rows.start, x.shape[1]
    part = x[rows].reshape(count, pixels // LANES, LANES).transpose(1, 0, 2)
    return part


def body(excitation, star_shell, star_pixel, star_fraction, star_count, observed, inverse_error):
    shells, pixels = excitation.shape
    devices = lax.axis_size("shell")
    me = lax.axis_index("shell")
    thickness = depth_span / (shells * devices)
    groups = pixels // LANES
    tall = shells + 1
    owners = star_shell.shape[1]

    up = [(i, i + 1) for i in range(devices - 1)]
    down = [(i + 1, i) for i in range(devices - 1)]
    from_below = lax.ppermute(edge_rows(excitation, slice(shells - PASSES, shells)), "shell", up)
    from_above = lax.ppermute(edge_rows(excitation, slice(0, PASSES)), "shell", down)
    owned = jnp.stack((observed[:, 0], inverse_error[:, 0]), axis=1)
    held = lax.all_to_all(owned, BOTH, split_axis=0, concat_axis=0, tiled=True)

    shell, pixel, fraction = star_shell[0], star_pixel[0], star_fraction[0]
    slot = lax.broadcasted_iota(jnp.int32, shell.shape, 1)
    low = pixel & (LANES - 1)
    row = (pixel >> 7) * tall + shell
    look_idx = (row << 7) | ((slot - low) & (LANES - 1))
    add_idx = (row << 7) | low
    alive = (slot < star_count[0][:, None]).astype(jnp.float32)

    edge = jnp.stack(((me > 0).astype(jnp.float32), (me < devices - 1).astype(jnp.float32)))
    dens, tab, block_sum = density_call(
        to_tiles(excitation),
        from_below.reshape(groups * PASSES, LANES),
        from_above.reshape(groups * PASSES, LANES),
        edge, shells, groups, thickness)

    offset = exclusive_sums(block_sum, False)
    half = owners // 2
    col_a = lookup_call(look_idx, tab, fraction, 0, half)
    col_b = lookup_call(look_idx, tab, fraction, half, owners - half)

    residual, here, inner, tail = star_call(
        pixel, offset, col_a, col_b, fraction, alive, held[:, 0], held[:, 1])
    tail_offset = exclusive_sums(tail, True)
    residual = lax.all_to_all(residual[:, None, :], BOTH, split_axis=0, concat_axis=0, tiled=True)

    rows = groups * tall + SPARE
    drop = spread_call(add_idx, here, inner, rows, 0, half)
    drop = spread_call(add_idx, here, inner, rows, half, owners - half, drop)
    extinction = extinction_call(tab, offset, shells)
    sensitivity = sensitivity_call(dens, drop, tail_offset, shells)
    return from_tiles(extinction), from_tiles(sensitivity), residual


def solution(mesh):
    placed = (
        P("shell", "sky"),
        P(BOTH, None, None),
        P(BOTH, None, None),
        P(BOTH, None, None),
        P(BOTH, None),
        P(None, BOTH, None),
        P(None, BOTH, None),
    )
    return jax.shard_map(
        body,
        mesh=mesh,
        in_specs=placed,
        out_specs=(P("shell", "sky"), P("shell", "sky"), P(None, BOTH, None)),
        check_vma=False,
    )
```

time: 864 us -> 226 us (0.26)
  the two profiles are of different devices: /device:TPU:1 before, /device:TPU:87 now
where the time goes in v1:
time: 226 us; the launch traced here: 223 us
  Pallas kernels  128 us (57%)
  starting transfers between devices  62 us (27%)
  blocking collectives  14 us (6%)
  waiting for transfers between devices  7.01 us (3%)
  local copies, waits for them, and re-layouts  5.87 us (3%)
  other arithmetic  5.21 us (2%)
    pallas_call x2, Pallas kernels, spread_call(): pl.pallas_call(lambda *refs: spread_kernel(first, count, start is not Non...  48.8 us
    pallas_call x2, Pallas kernels, lookup_call(): pl.pallas_call(lambda *refs: lookup_kernel(first, *refs), out_shape=jax.S...  37 us
    all_to_all x3, starting transfers between devices, exclusive_sums(): lax.all_to_all(parts, 'shell', split_axis=0, concat_axis=0, tiled=True)  33.5 us
    pallas_call x1, Pallas kernels, star_call(): pl.pallas_call(star_kernel, out_shape=[slots, slots, slots, jax.ShapeDtyp...  15 us
    all_to_all x1, blocking collectives, exclusive_sums(): lax.all_to_all(parts, 'shell', split_axis=0, concat_axis=0, tiled=True)  14 us
    all_to_all x1, starting transfers between devices, body(): lax.all_to_all(residual[:, None, :], BOTH, split_axis=0, concat_axis=0, t...  13 us
    all_to_all x1, starting transfers between devices, body(): held = lax.all_to_all(owned, BOTH, split_axis=0, concat_axis=0, tiled=True)  10.2 us
    pallas_call x1, Pallas kernels, density_call(): pl.pallas_call(lambda *refs: density_kernel(shells, thickness, *refs), gr...  8.9 us
  transfers between devices with their start and end apart: 7, of which 2 were waited for; matrix products, arithmetic and copies ran while one was open for 3% of the time, Pallas kernels for 42%

profile of v1, /device:TPU:87, one launch (start us, length us, event | category | flops | bytes accessed | tf_op | source)
XLA Modules:
  0.0 222.5 jit_solution(3246447318536598529)
XLA Ops:
  0.6 1.6 pad_maximum_fusion
  2.3 10.2 %all-to-all-start.2 = ((f32[128,2,128]{2,1,0:T(2,128)}), f32[128,2,128]{2,1,0:T(2,128)S(1)}, u32[]{:S(2)}, u32[]{:S(2)}) async-start(f32[128,2,128]{2,1,0:T(2,128)} %pad_maximum_fusion), calls=%async_computation.2 | async-start | bytes 262144 | tf_op jit(solution)/shard_map/all_to_all | solution.py:381
  12.5 1.7 slice_bitcast_fusion
  14.2 1.9 collective-permute-start.1
  16.1 3.4 %collective-permute-start = (f32[256,4,128]{2,1,0:T(4,128)S(1)}, f32[256,4,128]{2,1,0:T(4,128)S(1)}, u32[]{:S(2)}, u32[]{:S(2)}) collective-permute-start(f32[256,4,128]{2,1,0:T(4,128)S(1)} %get-tuple-element.21), channel_id=1, source_target_pairs={{0,2},{2,4},{4,6},{6,8},{8,10},{10,12},{12,14},{14,16},{16,18},{18... | collective-permute-start | bytes 1572872 | tf_op jit(solution)/shard_map/ppermute | solution.py:378
  19.5 1.6 and_or_fusion
  21.1 1.4 fusion.1.alive_ref
  22.4 0.6 add_convert_fusion.refs_0_
  23.1 0.0 all-to-all-done.2
  23.1 0.8 fusion.2
  23.9 5.3 %collective-permute-done.1 = f32[256,4,128]{2,1,0:T(4,128)S(1)} collective-permute-done((f32[256,4,128]{2,1,0:T(4,128)S(1)}, f32[256,4,128]{2,1,0:T(4,128)S(1)}, u32[]{:S(2)}, u32[]{:S(2)}) %collective-permute-start.1) | collective-permute-done | bytes 524320 | tf_op jit(solution)/shard_map/ppermute | solution.py:379
  29.2 1.6 collective-permute-done
  30.9 0.8 copy-done.4
  31.6 8.9 %density.1 = (f32[8192,128]{1,0:T(8,128)}, f32[8456,128]{1,0:T(8,128)}, f32[256,128]{1,0:T(8,128)}) custom-call(f32[2]{0:T(128)} %add_convert_fusion.refs_0_, f32[4,2048,128]{2,1,0:T(8,128)} %bitcast.58, f32[1024,128]{1,0:T(8,128)} %bitcast.67, f32[1024,128]{1,0:T(8,128)} %bitcast.66), custom_call_target="tpu_custom_call" | custom-call | flops 1600000000 | bytes 12582912 | tf_op jit(solution)/shard_map/density/pallas_call | solution.py:72
  40.6 14.0 %all-to-all-start = ((f32[64,4,128]{2,1,0:T(4,128)}), f32[64,4,128]{2,1,0:T(4,128)S(1)}, u32[]{:S(2)}, u32[]{:S(2)}) async-start(f32[64,4,128]{2,1,0:T(4,128)} %bitcast.59), calls=%async_computation | async-start | bytes 262144 | tf_op jit(solution)/shard_map/all_to_all | solution.py:150
  54.5 18.5 %lookup.3.col_b_ref = f32[64,128]{1,0:T(8,128)} custom-call(s32[128,128]{1,0:T(8,128)} %get-tuple-element.24.refs_0_, f32[8456,128]{1,0:T(8,128)} %get-tuple-element.10.refs_0_.refs_1_, f32[128,128]{1,0:T(8,128)} %bitcast.68), custom_call_target="tpu_custom_call" | custom-call | flops 3400000000 | bytes 5242880 | tf_op jit(solution)/shard_map/lookup/pallas_call | solution.py:115
  73.1 0.7 copy-done.2
  73.7 1.6 scan.2
  75.3 9.8 %all-to-all-start.1 = ((f32[64,4,128]{2,1,0:T(4,128)}), f32[64,4,128]{2,1,0:T(4,128)S(1)}, u32[]{:S(2)}, u32[]{:S(2)}) async-start(f32[64,4,128]{2,1,0:T(4,128)} %scan.2), calls=%async_computation.1 | async-start | bytes 262144 | tf_op jit(solution)/shard_map/all_to_all | solution.py:152
  85.1 18.5 %lookup.2.col_a_ref = f32[64,128]{1,0:T(8,128)} custom-call(s32[128,128]{1,0:T(8,128)} %get-tuple-element.24.refs_0_, f32[8456,128]{1,0:T(8,128)} %get-tuple-element.10.refs_0_.refs_1_, f32[128,128]{1,0:T(8,128)} %bitcast.69), custom_call_target="tpu_custom_call" | custom-call | flops 3400000000 | bytes 5242880 | tf_op jit(solution)/shard_map/lookup/pallas_call | solution.py:115
  103.6 0.7 copy-done
  104.3 15.0 %star.1 = (f32[128,128]{1,0:T(8,128)}, f32[128,128]{1,0:T(8,128)}, f32[128,128]{1,0:T(8,128)}, f32[256,128]{1,0:T(8,128)}) custom-call(s32[128,128]{1,0:T(8,128)} %bitcast.62, f32[256,128]{1,0:T(8,128)} %bitcast.55, f32[64,128]{1,0:T(8,128)} %lookup.2.col_a_ref, f32[64,128]{1,0:T(8,128)} %lookup.3.col_b_ref, f32[128,128]{1,0:T(8,128)} %bitcast.70, ...), custom_call_target="tpu_custom_call" | custom-call | flops 1600000000 | bytes 1048576 | tf_op jit(solution)/shard_map/star/pallas_call | solution.py:218
  119.3 14.0 %all_to_all.30.refs_0_ = f32[64,4,128]{2,1,0:T(4,128)} all-to-all(f32[64,4,128]{2,1,0:T(4,128)} %bitcast.60), channel_id=1, replica_groups=mesh['shell'=64,'sky'=2] {'shell'}, dimensions={0} | all-to-all | bytes 262144 | tf_op jit(solution)/shard_map/all_to_all | solution.py:150
  133.3 13.0 %all-to-all-start.5 = ((f32[128,1,128]{2,1,0:T(1,128)}), f32[128,1,128]{2,1,0:T(1,128)S(1)}, u32[]{:S(2)}, u32[]{:S(2)}) async-start(f32[128,1,128]{2,1,0:T(1,128)} %bitcast.61), calls=%async_computation.5 | async-start | bytes 131072 | tf_op jit(solution)/shard_map/all_to_all | solution.py:406
  146.3 24.4 %spread.2.refs_3_ = f32[8456,128]{1,0:T(8,128)} custom-call(s32[128,128]{1,0:T(8,128)} %get-tuple-element.25.refs_0_, f32[128,128]{1,0:T(8,128)} %get-tuple-element.13.refs_1_, f32[128,128]{1,0:T(8,128)} %get-tuple-element.14.refs_2_), custom_call_target="tpu_custom_call" | custom-call | flops 4000000000 | bytes 5242880 | tf_op jit(solution)/shard_map/spread/pallas_call | solution.py:281
  170.6 1.6 scan.3
  172.3 9.8 %all-to-all-start.4 = ((f32[64,4,128]{2,1,0:T(4,128)}), f32[64,4,128]{2,1,0:T(4,128)S(1)}, u32[]{:S(2)}, u32[]{:S(2)}) async-start(f32[64,4,128]{2,1,0:T(4,128)} %scan.3), calls=%async_computation.4 | async-start | bytes 262144 | tf_op jit(solution)/shard_map/all_to_all | solution.py:152
  182.1 24.4 %spread.3.refs_1_ = f32[8456,128]{1,0:T(8,128)} custom-call(s32[128,128]{1,0:T(8,128)} %get-tuple-element.25.refs_0_, f32[128,128]{1,0:T(8,128)} %get-tuple-element.13.refs_1_, f32[128,128]{1,0:T(8,128)} %get-tuple-element.14.refs_2_, f32[8456,128]{1,0:T(8,128)} %spread.2.refs_3_), custom_call_target="tpu_custom_call" | custom-call | flops 4000000000 | bytes 5242880 | tf_op jit(solution)/shard_map/spread/pallas_call | solution.py:281
  206.5 6.9 %extinction.1 = f32[4,2048,128]{2,1,0:T(8,128)} custom-call(f32[8456,128]{1,0:T(8,128)} %get-tuple-element.10.refs_0_.refs_1_, f32[256,128]{1,0:T(8,128)} %bitcast.56), custom_call_target="tpu_custom_call" | custom-call | flops 800000000 | bytes 8388608 | tf_op jit(solution)/shard_map/extinction/pallas_call | solution.py:305
  213.4 0.6 copy-done.1
  214.0 7.8 %sensitivity.1 = f32[4,2048,128]{2,1,0:T(8,128)} custom-call(f32[8192,128]{1,0:T(8,128)} %get-tuple-element.12.refs_0_, f32[8456,128]{1,0:T(8,128)} %spread.3.refs_1_, f32[256,128]{1,0:T(8,128)} %bitcast.57), custom_call_target="tpu_custom_call" | custom-call | flops 1000000000 | bytes 12582912 | tf_op jit(solution)/shard_map/sensitivity/pallas_call | solution.py:332
  221.9 0.6 copy.23
  (10 shorter events, 0.0 us)
Async XLA Ops:
  2.3 20.8 %all-to-all-start.2 = ((f32[128,2,128]{2,1,0:T(2,128)}), f32[128,2,128]{2,1,0:T(2,128)S(1)}, u32[]{:S(2)}, u32[]{:S(2)}) async-start(f32[128,2,128]{2,1,0:T(2,128)} %pad_maximum_fusion), calls=%async_computation.2 | async-start | bytes 262144 | tf_op jit(solution)/shard_map/all_to_all | solution.py:381
  14.2 15.0 %collective-permute-start.1 = (f32[256,4,128]{2,1,0:T(4,128)S(1)}, f32[256,4,128]{2,1,0:T(4,128)S(1)}, u32[]{:S(2)}, u32[]{:S(2)}) collective-permute-start(f32[256,4,128]{2,1,0:T(4,128)S(1)} %get-tuple-element.20), channel_id=1, source_target_pairs={{2,0},{4,2},{6,4},{8,6},{10,8},{12,10},{14,12},{16,14},{18,16},{20... | collective-permute-start | bytes 1572872 | tf_op jit(solution)/shard_map/ppermute | solution.py:379
  16.1 14.7 %collective-permute-start = (f32[256,4,128]{2,1,0:T(4,128)S(1)}, f32[256,4,128]{2,1,0:T(4,128)S(1)}, u32[]{:S(2)}, u32[]{:S(2)}) collective-permute-start(f32[256,4,128]{2,1,0:T(4,128)S(1)} %get-tuple-element.21), channel_id=1, source_target_pairs={{0,2},{2,4},{4,6},{6,8},{8,10},{10,12},{12,14},{14,16},{16,18},{18... | collective-permute-start | bytes 1572872 | tf_op jit(solution)/shard_map/ppermute | solution.py:378
  29.2 1.7 copy-start.3
  30.9 0.8 copy-start.4
  40.6 32.5 %all-to-all-start = ((f32[64,4,128]{2,1,0:T(4,128)}), f32[64,4,128]{2,1,0:T(4,128)S(1)}, u32[]{:S(2)}, u32[]{:S(2)}) async-start(f32[64,4,128]{2,1,0:T(4,128)} %bitcast.59), calls=%async_computation | async-start | bytes 262144 | tf_op jit(solution)/shard_map/all_to_all | solution.py:150
  73.1 0.7 copy-start.2
  75.3 28.3 %all-to-all-start.1 = ((f32[64,4,128]{2,1,0:T(4,128)}), f32[64,4,128]{2,1,0:T(4,128)S(1)}, u32[]{:S(2)}, u32[]{:S(2)}) async-start(f32[64,4,128]{2,1,0:T(4,128)} %scan.2), calls=%async_computation.1 | async-start | bytes 262144 | tf_op jit(solution)/shard_map/all_to_all | solution.py:152
  103.6 0.7 copy-start
  133.3 39.0 %all-to-all-start.5 = ((f32[128,1,128]{2,1,0:T(1,128)}), f32[128,1,128]{2,1,0:T(1,128)S(1)}, u32[]{:S(2)}, u32[]{:S(2)}) async-start(f32[128,1,128]{2,1,0:T(1,128)} %bitcast.61), calls=%async_computation.5 | async-start | bytes 131072 | tf_op jit(solution)/shard_map/all_to_all | solution.py:406
  172.3 41.1 %all-to-all-start.4 = ((f32[64,4,128]{2,1,0:T(4,128)}), f32[64,4,128]{2,1,0:T(4,128)S(1)}, u32[]{:S(2)}, u32[]{:S(2)}) async-start(f32[64,4,128]{2,1,0:T(4,128)} %scan.3), calls=%async_computation.4 | async-start | bytes 262144 | tf_op jit(solution)/shard_map/all_to_all | solution.py:152
  213.4 0.6 copy-start.1

commit v2 on v1

v2 whole, which is shorter than its diff:
```python
import jax
import jax.numpy as jnp
from jax import lax
from jax.experimental import pallas as pl
from jax.experimental.pallas import tpu as pltpu
from jax.sharding import PartitionSpec as P

PASSES = 4
LANES = 128
SUB = 8
LEAD = 8
ACCS = 4
CHUNKS = 8
SPLIT = 7
PACK = 64
FIELDS = 4
BOTH = ("shell", "sky")


depth_span = 2.0

VMEM = pl.BlockSpec(memory_space=pltpu.VMEM)
SMEM = pl.BlockSpec(memory_space=pltpu.SMEM)
ANY = pl.BlockSpec(memory_space=pl.ANY)


def cost(micros, nbytes):
    return pl.CostEstimate(flops=int(micros * 2e8), bytes_accessed=int(nbytes), transcendentals=0)


def taps():
    power = [1.0]
    total = [0.0] * (2 * PASSES + 1)
    for k in range(PASSES + 1):
        for i, v in enumerate(power):
            total[PASSES - k + i] += v
        wider = [0.0] * (len(power) + 2)
        for i, v in enumerate(power):
            wider[i] += 0.3 * v
            wider[i + 1] += 0.35 * v
            wider[i + 2] += 0.3 * v
        power = wider
    return total[PASSES:]


def table_rows(groups, tall):
    unit = SPLIT * PACK
    return -(-(LEAD + groups * tall + SUB) // unit) * unit


def density_kernel(shells, groups, devices, thickness, edge_ref, obs_ref, inv_ref, exc_hbm, up_hbm, down_hbm,
                   dens_hbm, tab_hbm, pay_ref, exc_ref, up_ref, down_ref, dens_ref, tab_ref, in_sem, out_sem):
    tall = shells + 1
    per = groups // CHUNKS
    weight = taps()
    low_edge = edge_ref[0]
    high_edge = edge_ref[1]

    def inputs(i):
        wide = pl.ds(i * per * SUB, per * SUB)
        thin = pl.ds(i * per * PASSES, per * PASSES)
        return [
            pltpu.make_async_copy(exc_hbm.at[:, wide, :], exc_ref.at[:, wide, :], in_sem.at[0, i]),
            pltpu.make_async_copy(up_hbm.at[thin, :], up_ref.at[thin, :], in_sem.at[1, i]),
            pltpu.make_async_copy(down_hbm.at[thin, :], down_ref.at[thin, :], in_sem.at[2, i]),
        ]

    def outputs(i):
        flat = pl.ds(i * per * shells, per * shells)
        tall_rows = pl.ds(LEAD + i * per * tall, per * tall)
        return [
            pltpu.make_async_copy(dens_ref.at[flat, :], dens_hbm.at[flat, :], out_sem.at[0, i]),
            pltpu.make_async_copy(tab_ref.at[tall_rows, :], tab_hbm.at[tall_rows, :], out_sem.at[1, i]),
        ]

    for i in range(CHUNKS):
        for copy in inputs(i):
            copy.start()
    pay_ref[pl.ds(0, devices, stride=FIELDS), :] = obs_ref[...]
    pay_ref[pl.ds(1, devices, stride=FIELDS), :] = inv_ref[...]

    def group(g):
        exc = {}
        for r in range(shells):
            exc[r] = exc_ref.at[r // SUB][pl.ds(g * SUB * SUB + r % SUB, SUB, stride=SUB), :]
        for k in range(PASSES):
            low = up_ref[pl.ds(g * SUB * PASSES + PASSES - 1 - k, SUB, stride=PASSES), :]
            high = down_ref[pl.ds(g * SUB * PASSES + k, SUB, stride=PASSES), :]
            if k:
                low = low - low_edge * exc[k - 1]
                high = high - high_edge * exc[shells - k]
            exc[-1 - k] = low
            exc[shells + k] = high
        tab_ref[pl.ds(LEAD + g * SUB * tall, SUB, stride=tall), :] = jnp.zeros((SUB, LANES), jnp.float32)
        total = None
        for r in range(shells):
            value = weight[0] * exc[r]
            for k in range(1, PASSES + 1):
                value = value + weight[k] * (exc[r - k] + exc[r + k])
            dens = jnp.exp(value)
            dens_ref[pl.ds((g * shells + r) * SUB, SUB), :] = dens
            step = dens * thickness
            total = step if total is None else total + step
            tab_ref[pl.ds(LEAD + g * SUB * tall + 1 + r, SUB, stride=tall), :] = total
        first = g * SUB
        pay_ref[pl.ds((first % devices) * FIELDS + 2 + first // devices, SUB, stride=FIELDS), :] = total

    def chunk(i, carry):
        for copy in inputs(i):
            copy.wait()
        for k in range(per // SUB):
            group(i * (per // SUB) + k)
        for copy in outputs(i):
            copy.start()
        return carry

    lax.fori_loop(0, CHUNKS, chunk, 0)
    for i in range(CHUNKS):
        for copy in outputs(i):
            copy.wait()


def density_call(exc, up, down, edge, obs, inv, shells, groups, devices, thickness):
    tall = shells + 1
    rows = table_rows(groups, tall)
    return pl.pallas_call(
        lambda *refs: density_kernel(shells, groups, devices, thickness, *refs),
        in_specs=[SMEM, VMEM, VMEM, ANY, ANY, ANY],
        out_specs=[ANY, ANY, VMEM],
        out_shape=[
            jax.ShapeDtypeStruct((groups * shells, LANES), jnp.float32),
            jax.ShapeDtypeStruct((rows, LANES), jnp.float32),
            jax.ShapeDtypeStruct((devices * FIELDS, LANES), jnp.float32),
        ],
        scratch_shapes=[
            pltpu.VMEM(exc.shape, jnp.float32),
            pltpu.VMEM(up.shape, jnp.float32),
            pltpu.VMEM(down.shape, jnp.float32),
            pltpu.VMEM((groups * shells, LANES), jnp.float32),
            pltpu.VMEM((rows, LANES), jnp.float32),
            pltpu.SemaphoreType.DMA((3, CHUNKS)),
            pltpu.SemaphoreType.DMA((2, CHUNKS)),
        ],
        cost_estimate=cost(8, 12 << 20),
        name="density",
    )(edge, obs, inv, exc, up, down)


def lookup_kernel(first, idx_ref, tab_ref, low_ref, frac_ref, out_ref):
    lane = lax.broadcasted_iota(jnp.int32, (SUB, LANES), 1)
    sub = lax.broadcasted_iota(jnp.int32, (SUB, LANES), 0)
    pair = [(sub >> 1) == j for j in range(4)]
    quad = lane >> 2
    is_inner = sub == (lane & 3) * 2
    is_outer = sub == (lane & 3) * 2 + 1

    def body(o, carry):
        low = jnp.broadcast_to(low_ref[pl.ds(o + first, 1), :], (SUB, LANES))
        got = jnp.zeros((SUB, LANES), jnp.float32)
        for k in range(LANES // 4):
            rows = tab_ref[pl.ds(idx_ref[o + first, 4 * k], SUB), :]
            for j in range(1, 4):
                rows = jnp.where(pair[j], tab_ref[pl.ds(idx_ref[o + first, 4 * k + j] - 2 * j, SUB), :], rows)
            got = jnp.where(quad == k, jnp.take_along_axis(rows, low, axis=1), got)
        inner = jnp.sum(jnp.where(is_inner, got, 0.0), axis=0, keepdims=True)
        outer = jnp.sum(jnp.where(is_outer, got, 0.0), axis=0, keepdims=True)
        out_ref[pl.ds(o, 1), :] = inner + frac_ref[pl.ds(o + first, 1), :] * (outer - inner)
        return carry

    lax.fori_loop(0, out_ref.shape[0], body, 0)


def lookup_call(idx, tab, low, frac, first, count):
    return pl.pallas_call(
        lambda *refs: lookup_kernel(first, *refs),
        out_shape=jax.ShapeDtypeStruct((count, LANES), jnp.float32),
        in_specs=[SMEM, VMEM, VMEM, VMEM],
        out_specs=VMEM,
        cost_estimate=cost(15, 5 << 20),
        name="lookup",
    )(idx, tab, low, frac)


def scan_kernel(reverse, in_ref, out_ref, *field_ref):
    blocks = in_ref.shape[0] // SUB
    total = jnp.zeros((SUB, LANES), jnp.float32)
    for b in range(blocks - 1, -1, -1) if reverse else range(blocks):
        out_ref[4 * b:4 * b + 2, :] = total[2:4]
        out_ref[4 * b + 2:4 * b + 4, :] = total[6:8]
        total = total + in_ref[SUB * b:SUB * (b + 1), :]
    if field_ref:
        field_ref[0][...] = in_ref[pl.ds(0, field_ref[0].shape[0], stride=FIELDS), :]


def scan_call(parts, devices, reverse, field):
    shapes = [jax.ShapeDtypeStruct((devices * (FIELDS - 2), LANES), jnp.float32)]
    if field:
        shapes.append(jax.ShapeDtypeStruct((devices, LANES), jnp.float32))
    return pl.pallas_call(
        lambda *refs: scan_kernel(reverse, *refs),
        out_shape=shapes,
        cost_estimate=cost(1, 1 << 18),
        name="scan",
    )(parts)


def exchange(rows, devices):
    parts = rows.reshape(devices, rows.shape[0] // devices, LANES)
    parts = lax.all_to_all(parts, BOTH, split_axis=0, concat_axis=0, tiled=True)
    return parts.reshape(rows.shape)


def halves(x):
    high = x.astype(jnp.bfloat16)
    return high, (x - high.astype(jnp.float32)).astype(jnp.bfloat16)


def star_kernel(devices, count_ref, pix_ref, off_ref, held_ref, col_a_ref, col_b_ref, frac_ref,
                pay_ref, here_ref, inner_ref, acc_ref, tail_ref):
    groups = off_ref.shape[0]
    rows = SUB
    offt = jnp.transpose(off_ref[...])
    offt = jnp.concatenate(halves(offt), axis=0)
    group_id = lax.broadcasted_iota(jnp.int32, (groups, LANES), 0).astype(jnp.bfloat16)
    lane_id = lax.broadcasted_iota(jnp.int32, (LANES, LANES), 0)
    slot = lax.broadcasted_iota(jnp.int32, (rows, LANES), 1)
    sub = lax.broadcasted_iota(jnp.int32, (rows, LANES), 0)
    one = jnp.ones((groups, LANES), jnp.bfloat16)
    zero = jnp.zeros((groups, LANES), jnp.bfloat16)
    acc_ref[...] = jnp.zeros_like(acc_ref)
    pay_ref[pl.ds(1, devices, stride=FIELDS), :] = jnp.zeros((devices, LANES), jnp.float32)

    def body(b, col_ref, shift):
        at = pl.ds(pl.multiple_of(b * rows, rows), rows)
        local = pl.ds(pl.multiple_of((b - shift) * rows, rows), rows)
        pix = pix_ref[at, :]
        high = lax.shift_right_logical(pix, 7)
        high = (lax.rem(high, devices)) * (groups // devices) + lax.div(high, devices)
        high = high.astype(jnp.float32).astype(jnp.bfloat16)
        low = pix & 127
        pick = jnp.concatenate([jnp.where(group_id == high[j:j + 1, :], one, zero) for j in range(rows)], axis=1)
        found = jnp.dot(offt, pick, preferred_element_type=jnp.float32)
        lanes = [lane_id == low[j:j + 1, :] for j in range(rows)]
        off_at = []
        for j in range(rows):
            part = found[:, j * LANES:(j + 1) * LANES]
            part = jnp.where(lanes[j], part[:LANES] + part[LANES:], 0.0)
            off_at.append(jnp.sum(part, axis=0, keepdims=True))
        column = col_ref[local, :] + jnp.concatenate(off_at, axis=0)
        transmit = jnp.exp(-column)
        obs = held_ref[pl.ds(b * rows * FIELDS, rows, stride=FIELDS), :]
        inv = held_ref[pl.ds(b * rows * FIELDS + 1, rows, stride=FIELDS), :]
        live = jnp.zeros((rows, LANES), jnp.int32)
        for j in range(rows):
            live = jnp.where(sub == j, count_ref[0, b * rows + j], live)
        residual = jnp.where(slot < live, (obs - (1.0 - transmit)) * inv, 0.0)
        pull = -residual * inv * transmit
        inner = (1.0 - frac_ref[at, :]) * pull
        pay_ref[pl.ds(b * rows * FIELDS, rows, stride=FIELDS), :] = residual
        here_ref[at, :] = pull - inner
        inner_ref[at, :] = inner
        spread = []
        for j in range(rows):
            spread.append(jnp.concatenate(halves(jnp.where(lanes[j], pull[j:j + 1, :], 0.0)), axis=0))
        spread = jnp.concatenate(spread, axis=1)
        acc_ref[...] += lax.dot_general(
            pick, spread, (((1,), (1,)), ((), ())), preferred_element_type=jnp.float32)

    half = col_a_ref.shape[0] // rows
    full = pix_ref.shape[0] // rows

    @pl.loop(0, half)
    def _(b):
        body(b, col_a_ref, 0)

    @pl.loop(half, full)
    def _(b):
        body(b, col_b_ref, half)

    tail_ref[...] = acc_ref[:, :LANES] + acc_ref[:, LANES:]
    for e in range(groups // devices):
        pay_ref[pl.ds(2 + e, devices, stride=FIELDS), :] = tail_ref[pl.ds(e, devices, stride=groups // devices), :]


def star_call(count, pix, off, held, col_a, col_b, frac, devices):
    slots = jax.ShapeDtypeStruct(pix.shape, jnp.float32)
    return pl.pallas_call(
        lambda *refs: star_kernel(devices, *refs),
        out_shape=[jax.ShapeDtypeStruct(held.shape, jnp.float32), slots, slots],
        in_specs=[SMEM] + [VMEM] * 6,
        out_specs=[VMEM] * 3,
        scratch_shapes=[pltpu.VMEM((off.shape[0], 2 * LANES), jnp.float32), pltpu.VMEM(off.shape, jnp.float32)],
        cost_estimate=cost(8, 1 << 20),
        name="star",
    )(count, pix, off, held, col_a, col_b, frac)


def spread_kernel(first, count, start, idx_ref, low_ref, here_ref, inner_ref, *refs):
    if start:
        start_hbm, refs = refs[0], refs[1:]
    out_hbm = refs[0]
    accs = refs[1:1 + ACCS]
    sem = refs[1 + ACCS]
    total_rows = out_hbm.shape[0]
    piece = total_rows // SPLIT

    if start:
        begin = pltpu.make_async_copy(start_hbm, accs[0], sem.at[SPLIT])
        begin.start()

    def clear(i, carry):
        for acc in accs[1 if start else 0:]:
            acc[pl.ds(pl.multiple_of(i * PACK, PACK), PACK), :] = jnp.zeros((PACK, LANES), jnp.float32)
        return carry

    lax.fori_loop(0, total_rows // PACK, clear, 0)
    if start:
        begin.wait()
    lane = lax.broadcasted_iota(jnp.int32, (SUB, LANES), 1)
    sub = lax.broadcasted_iota(jnp.int32, (SUB, LANES), 0)
    pair = sub >> 1
    in_pair = [pair == j for j in range(4)]
    even = (sub & 1) == 0

    def body(o, carry):
        def row_of(ref):
            return jnp.broadcast_to(ref[pl.ds(o, 1), :], (SUB, LANES))

        low = row_of(low_ref)
        value = jnp.where(even, row_of(inner_ref), row_of(here_ref))
        for k in range(LANES // 4):
            at = pair + 4 * k
            here = jnp.take_along_axis(low, at, axis=1) == lane
            four = jnp.where(here, jnp.take_along_axis(value, at, axis=1), 0.0)
            for j in range(4):
                acc = accs[(4 * k + j) % ACCS]
                rows = pl.ds(idx_ref[o, 4 * k + j] - 2 * j, SUB)
                acc[rows, :] = acc[rows, :] + jnp.where(in_pair[j], four, 0.0)
        return carry

    lax.fori_loop(first, first + count, body, 0)

    copies = []
    for i in range(SPLIT):
        def gather(k, carry, i=i):
            rows = pl.ds(pl.multiple_of(i * piece + k * PACK, PACK), PACK)
            total = accs[0][rows, :]
            for acc in accs[1:]:
                total = total + acc[rows, :]
            accs[0][rows, :] = total
            return carry

        lax.fori_loop(0, piece // PACK, gather, 0)
        part = pl.ds(i * piece, piece)
        copy = pltpu.make_async_copy(accs[0].at[part, :], out_hbm.at[part, :], sem.at[i])
        copy.start()
        copies.append(copy)
    for copy in copies:
        copy.wait()


def spread_call(idx, low, here, inner, rows, first, count, start=None):
    shape = (rows, LANES)
    extra = () if start is None else (start,)
    return pl.pallas_call(
        lambda *refs: spread_kernel(first, count, start is not None, *refs),
        out_shape=jax.ShapeDtypeStruct(shape, jnp.float32),
        in_specs=[SMEM, VMEM, VMEM, VMEM] + [ANY] * len(extra),
        out_specs=ANY,
        scratch_shapes=[pltpu.VMEM(shape, jnp.float32)] * ACCS + [pltpu.SemaphoreType.DMA((SPLIT + 1,))],
        cost_estimate=cost(20, 5 << 20),
        name="spread",
    )(idx, low, here, inner, *extra)


def chunked(work, inputs, outputs):
    for i in range(CHUNKS):
        for copy in inputs(i):
            copy.start()

    def step(i, carry):
        for copy in inputs(i):
            copy.wait()
        work(i)
        for copy in outputs(i):
            copy.start()
        return carry

    lax.fori_loop(0, CHUNKS, step, 0)
    for i in range(CHUNKS):
        for copy in outputs(i):
            copy.wait()


def extinction_kernel(shells, devices, off_ref, tab_hbm, out_hbm, tab_ref, out_ref, in_sem, out_sem):
    tall = shells + 1
    groups = off_ref.shape[0]
    per = groups // CHUNKS

    def inputs(i):
        rows = pl.ds(LEAD + i * per * tall, per * tall)
        return [pltpu.make_async_copy(tab_hbm.at[rows, :], tab_ref.at[rows, :], in_sem.at[i])]

    def outputs(i):
        rows = pl.ds(i * per * SUB, per * SUB)
        return [pltpu.make_async_copy(out_ref.at[:, rows, :], out_hbm.at[:, rows, :], out_sem.at[i])]

    def work(i):
        for k in range(per):
            g = i * per + k
            off = off_ref[pl.ds((g % devices) * (groups // devices) + g // devices, 1), :]
            for b in range(shells // SUB):
                value = tab_ref[pl.ds(LEAD + g * tall + 1 + b * SUB, SUB), :] + off
                out_ref[b, pl.ds(pl.multiple_of(g * SUB, SUB), SUB), :] = value

    chunked(work, inputs, outputs)


def extinction_call(tab, off, shells, devices):
    shape = (shells // SUB, off.shape[0] * SUB, LANES)
    return pl.pallas_call(
        lambda *refs: extinction_kernel(shells, devices, *refs),
        in_specs=[VMEM, ANY],
        out_specs=ANY,
        out_shape=jax.ShapeDtypeStruct(shape, jnp.float32),
        scratch_shapes=[
            pltpu.VMEM(tab.shape, jnp.float32),
            pltpu.VMEM(shape, jnp.float32),
            pltpu.SemaphoreType.DMA((CHUNKS,)),
            pltpu.SemaphoreType.DMA((CHUNKS,)),
        ],
        cost_estimate=cost(4, 8 << 20),
        name="extinction",
    )(off, tab)


def sensitivity_kernel(shells, devices, off_ref, dens_hbm, drop_hbm, out_hbm, dens_ref, drop_ref, out_ref,
                       in_sem, out_sem):
    tall = shells + 1
    groups = off_ref.shape[0]
    share = groups // devices
    per = groups // CHUNKS

    def inputs(i):
        flat = pl.ds(i * per * shells, per * shells)
        rows = pl.ds(LEAD + i * per * tall, per * tall)
        return [
            pltpu.make_async_copy(dens_hbm.at[flat, :], dens_ref.at[flat, :], in_sem.at[0, i]),
            pltpu.make_async_copy(drop_hbm.at[rows, :], drop_ref.at[rows, :], in_sem.at[1, i]),
        ]

    def outputs(i):
        rows = pl.ds(i * per * SUB, per * SUB)
        return [pltpu.make_async_copy(out_ref.at[:, rows, :], out_hbm.at[:, rows, :], out_sem.at[i])]

    def work(i):
        for k in range(per // SUB):
            g = i * (per // SUB) + k
            first = g * SUB
            total = off_ref[pl.ds((first % devices) * share + first // devices, SUB, stride=share), :]
            for r in range(shells - 1, -1, -1):
                total = total + drop_ref[pl.ds(LEAD + g * SUB * tall + 1 + r, SUB, stride=tall), :]
                out_ref.at[r // SUB][pl.ds(g * SUB * SUB + r % SUB, SUB, stride=SUB), :] = (
                    dens_ref[pl.ds((g * shells + r) * SUB, SUB), :] * total)

    chunked(work, inputs, outputs)


def sensitivity_call(dens, drop, off, shells, devices):
    shape = (shells // SUB, off.shape[0] * SUB, LANES)
    return pl.pallas_call(
        lambda *refs: sensitivity_kernel(shells, devices, *refs),
        in_specs=[VMEM, ANY, ANY],
        out_specs=ANY,
        out_shape=jax.ShapeDtypeStruct(shape, jnp.float32),
        scratch_shapes=[
            pltpu.VMEM(dens.shape, jnp.float32),
            pltpu.VMEM(drop.shape, jnp.float32),
            pltpu.VMEM(shape, jnp.float32),
            pltpu.SemaphoreType.DMA((2, CHUNKS)),
            pltpu.SemaphoreType.DMA((CHUNKS,)),
        ],
        cost_estimate=cost(5, 12 << 20),
        name="sensitivity",
    )(off, dens, drop)


def to_tiles(x):
    shells, pixels = x.shape
    groups = pixels // LANES
    x = x.reshape(shells // SUB, SUB, groups, LANES).transpose(0, 2, 1, 3)
    return x.reshape(shells // SUB, groups * SUB, LANES)


def from_tiles(x):
    bands, rows, lanes = x.shape
    groups = rows // SUB
    x = x.reshape(bands, groups, SUB, lanes).transpose(0, 2, 1, 3)
    return x.reshape(bands * SUB, groups * lanes)


def edge_rows(x, rows):
    count, pixels = rows.stop - rows.start, x.shape[1]
    part = x[rows].reshape(count, pixels // LANES, LANES).transpose(1, 0, 2)
    return part


def body(excitation, star_shell, star_pixel, star_fraction, star_count, observed, inverse_error):
    shells, pixels = excitation.shape
    blocks = lax.axis_size("shell")
    devices = blocks * lax.axis_size("sky")
    me = lax.axis_index("shell")
    thickness = depth_span / (shells * blocks)
    groups = pixels // LANES
    tall = shells + 1
    owners = star_shell.shape[1]

    up = [(i, i + 1) for i in range(blocks - 1)]
    down = [(i + 1, i) for i in range(blocks - 1)]
    from_below = lax.ppermute(edge_rows(excitation, slice(shells - PASSES, shells)), "shell", up)
    from_above = lax.ppermute(edge_rows(excitation, slice(0, PASSES)), "shell", down)

    pixel, fraction = star_pixel[0], star_fraction[0]
    low = pixel & (LANES - 1)
    idx = (pixel >> 7) * tall + star_shell[0] + LEAD
    edge = jnp.stack(((me == 0).astype(jnp.float32), (me == blocks - 1).astype(jnp.float32)))
    dens, tab, parts = density_call(
        to_tiles(excitation),
        from_below.reshape(groups * PASSES, LANES),
        from_above.reshape(groups * PASSES, LANES),
        edge, observed[:, 0], inverse_error[:, 0], shells, groups, devices, thickness)

    held = exchange(parts, devices)
    offset = exchange(scan_call(held, devices, False, False)[0], devices)
    half = owners // 2
    col_a = lookup_call(idx, tab, low, fraction, 0, half)
    col_b = lookup_call(idx, tab, low, fraction, half, owners - half)

    parts, here, inner = star_call(star_count, pixel, offset, held, col_a, col_b, fraction, devices)
    sums, residual = scan_call(exchange(parts, devices), devices, True, True)
    tail_offset = exchange(sums, devices)

    rows = table_rows(groups, tall)
    drop = spread_call(idx, low, here, inner, rows, 0, half)
    drop = spread_call(idx, low, here, inner, rows, half, owners - half, drop)
    extinction = extinction_call(tab, offset, shells, devices)
    sensitivity = sensitivity_call(dens, drop, tail_offset, shells, devices)
    return from_tiles(extinction), from_tiles(sensitivity), residual[:, None, :]


def solution(mesh):
    placed = (
        P("shell", "sky"),
        P(BOTH, None, None),
        P(BOTH, None, None),
        P(BOTH, None, None),
        P(BOTH, None),
        P(None, BOTH, None),
        P(None, BOTH, None),
    )
    return jax.shard_map(
        body,
        mesh=mesh,
        in_specs=placed,
        out_specs=(P("shell", "sky"), P("shell", "sky"), P(None, BOTH, None)),
        check_vma=False,
    )
```

time: 226 us -> 177 us (0.78)
  Pallas kernels: 128 us -> 108 us
  blocking collectives: 14 us -> 0 us
  starting transfers between devices: 62 us -> 49.9 us
  other arithmetic: 5.21 us -> 2.14 us
    all_to_all x1 -> x0, blocking collectives: 14 us -> none  [exclusive_sums(): lax.all_to_all(parts, 'shell', split_axis=0, concat_axis=0, tiled=True)]
    all_to_all x5 -> x4, starting transfers between devices: 56.7 us -> 44.7 us  [exchange(): parts = lax.all_to_all(parts, BOTH, split_axis=0, concat_axis=0, tiled=True)]
    pallas_call x2, Pallas kernels: 37 us -> 29 us  [lookup_call(): pl.pallas_call(lambda *refs: lookup_kernel(first, *refs), out_shape=jax.S...]
    pallas_call x2, Pallas kernels: 48.8 us -> 42.5 us  [spread_call(): pl.pallas_call(lambda *refs: spread_kernel(first, count, start is not Non...]
    pallas_call x6, Pallas kernels: 41.9 us -> 36 us  [the longest x1 14.9 us: star_call(): pl.pallas_call(lambda *refs: star_kernel(devices, *refs), out_shape=[jax....]
  transfers between devices with their start and end apart: 7 -> 6, of which waited for: 2 -> 2; matrix products, arithmetic and copies ran while one was open for 3% -> 1% of each run, Pallas kernels for 42% -> 44%
where the time goes in v2:
time: 177 us; the launch traced here: 175 us
  Pallas kernels  108 us (61%)
  starting transfers between devices  49.9 us (28%)
  waiting for transfers between devices  9.09 us (5%)
  local copies, waits for them, and re-layouts  5.2 us (3%)
  other arithmetic  2.14 us (1%)
    all_to_all x4, starting transfers between devices, exchange(): parts = lax.all_to_all(parts, BOTH, split_axis=0, concat_axis=0, tiled=True)  44.7 us
    pallas_call x2, Pallas kernels, spread_call(): pl.pallas_call(lambda *refs: spread_kernel(first, count, start is not Non...  42.5 us
    pallas_call x2, Pallas kernels, lookup_call(): pl.pallas_call(lambda *refs: lookup_kernel(first, *refs), out_shape=jax.S...  29 us
    pallas_call x1, Pallas kernels, star_call(): pl.pallas_call(lambda *refs: star_kernel(devices, *refs), out_shape=[jax....  14.9 us
    ppermute x1, waiting for transfers between devices, body(): lax.ppermute(edge_rows(excitation, slice(0, PASSES)), 'shell', down)  7.26 us
    pallas_call x1, Pallas kernels, density_call(): pl.pallas_call(lambda *refs: density_kernel(shells, groups, devices, thic...  6.91 us
    pallas_call x1, Pallas kernels, sensitivity_call(): pl.pallas_call(lambda *refs: sensitivity_kernel(shells, devices, *refs),...  6.37 us
    pallas_call x1, Pallas kernels, extinction_call(): pl.pallas_call(lambda *refs: extinction_kernel(shells, devices, *refs), i...  4.48 us
  transfers between devices with their start and end apart: 6, of which 2 were waited for; matrix products, arithmetic and copies ran while one was open for 1% of the time, Pallas kernels for 44%

profile of v2, /device:TPU:87, one launch (start us, length us, event | category | flops | bytes accessed | tf_op | source)
XLA Modules:
  0.0 174.7 jit_solution(9914201413705566166)
XLA Ops:
  0.6 1.7 slice_bitcast_fusion
  2.4 1.9 %collective-permute-start.1 = (f32[256,4,128]{2,1,0:T(4,128)S(1)}, f32[256,4,128]{2,1,0:T(4,128)S(1)}, u32[]{:S(2)}, u32[]{:S(2)}) collective-permute-start(f32[256,4,128]{2,1,0:T(4,128)S(1)} %get-tuple-element.22), channel_id=1, source_target_pairs={{2,0},{4,2},{6,4},{8,6},{10,8},{12,10},{14,12},{16,14},{18,16},{20... | collective-permute-start | bytes 1572872 | tf_op jit(solution)/shard_map/ppermute | solution.py:521
  4.3 3.4 %collective-permute-start = (f32[256,4,128]{2,1,0:T(4,128)S(1)}, f32[256,4,128]{2,1,0:T(4,128)S(1)}, u32[]{:S(2)}, u32[]{:S(2)}) collective-permute-start(f32[256,4,128]{2,1,0:T(4,128)S(1)} %get-tuple-element.23), channel_id=1, source_target_pairs={{0,2},{2,4},{4,6},{6,8},{8,10},{10,12},{12,14},{14,16},{16,18},{18... | collective-permute-start | bytes 1572872 | tf_op jit(solution)/shard_map/ppermute | solution.py:520
  7.7 0.6 add_convert_fusion.refs_0_
  8.3 1.5 broadcast_and_fusion
  9.8 7.3 %collective-permute-done.1 = f32[256,4,128]{2,1,0:T(4,128)S(1)} collective-permute-done((f32[256,4,128]{2,1,0:T(4,128)S(1)}, f32[256,4,128]{2,1,0:T(4,128)S(1)}, u32[]{:S(2)}, u32[]{:S(2)}) %collective-permute-start.1) | collective-permute-done | bytes 524320 | tf_op jit(solution)/shard_map/ppermute | solution.py:521
  17.1 1.8 %collective-permute-done = f32[256,4,128]{2,1,0:T(4,128)S(1)} collective-permute-done((f32[256,4,128]{2,1,0:T(4,128)S(1)}, f32[256,4,128]{2,1,0:T(4,128)S(1)}, u32[]{:S(2)}, u32[]{:S(2)}) %collective-permute-start) | collective-permute-done | bytes 524320 | tf_op jit(solution)/shard_map/ppermute | solution.py:520
  18.9 0.0 copy-done.4
  18.9 0.8 copy-done.5
  19.7 6.9 %density.1 = (f32[8192,128]{1,0:T(8,128)}, f32[8512,128]{1,0:T(8,128)}, f32[512,128]{1,0:T(8,128)}) custom-call(f32[2]{0:T(128)} %add_convert_fusion.refs_0_, f32[128,128]{1,0:T(8,128)} %bitcast.64, f32[128,128]{1,0:T(8,128)} %bitcast.65, f32[4,2048,128]{2,1,0:T(8,128)} %bitcast.53, f32[1024,128]{1,0:T(8,128)} %bitcast.63, f32[1024,128]{1,0:T(8,128)} %bitcast.62), custom_call_target="tpu_custom_call" | custom-call | flops 1600000000 | bytes 12582912 | tf_op jit(solution)/shard_map/density/pallas_call | solution.py:126
  26.6 15.4 %all-to-all-start = ((f32[128,4,128]{2,1,0:T(4,128)}), f32[128,4,128]{2,1,0:T(4,128)S(1)}, u32[]{:S(2)}, u32[]{:S(2)}) async-start(f32[128,4,128]{2,1,0:T(4,128)} %bitcast.57), calls=%async_computation | async-start | bytes 524288 | tf_op jit(solution)/shard_map/all_to_all | solution.py:209
  42.0 14.5 %lookup.3.refs_5_ = f32[64,128]{1,0:T(8,128)} custom-call(s32[128,128]{1,0:T(8,128)} %get-tuple-element.25.refs_0_, f32[8512,128]{1,0:T(8,128)} %get-tuple-element.12.refs_1_, s32[128,128]{1,0:T(8,128)} %get-tuple-element.24.refs_2_.refs_1_, f32[128,128]{1,0:T(8,128)} %bitcast.66), custom_call_target="tpu_custom_call" | custom-call | flops 3000000000 | bytes 5242880 | tf_op jit(solution)/shard_map/lookup/pallas_call | solution.py:174
  56.5 0.0 all-to-all-done
  56.5 0.7 copy-done.2
  57.2 1.7 scan.2
  58.9 9.8 %all-to-all-start.1 = ((f32[128,2,128]{2,1,0:T(2,128)}), f32[128,2,128]{2,1,0:T(2,128)S(1)}, u32[]{:S(2)}, u32[]{:S(2)}) async-start(f32[128,2,128]{2,1,0:T(2,128)} %bitcast.60), calls=%async_computation.1 | async-start | bytes 262144 | tf_op jit(solution)/shard_map/all_to_all | solution.py:209
  68.7 14.5 %lookup.2.refs_4_ = f32[64,128]{1,0:T(8,128)} custom-call(s32[128,128]{1,0:T(8,128)} %get-tuple-element.25.refs_0_, f32[8512,128]{1,0:T(8,128)} %get-tuple-element.12.refs_1_, s32[128,128]{1,0:T(8,128)} %get-tuple-element.24.refs_2_.refs_1_, f32[128,128]{1,0:T(8,128)} %bitcast.67), custom_call_target="tpu_custom_call" | custom-call | flops 3000000000 | bytes 5242880 | tf_op jit(solution)/shard_map/lookup/pallas_call | solution.py:174
  83.2 0.0 all-to-all-done.1
  83.2 0.6 copy-done
  83.8 14.9 %star.1 = (f32[512,128]{1,0:T(8,128)}, f32[128,128]{1,0:T(8,128)}, f32[128,128]{1,0:T(8,128)}) custom-call(s32[1,128]{1,0:T(1,128)} %refs_0_.1, s32[128,128]{1,0:T(8,128)} %bitcast.61, f32[256,128]{1,0:T(8,128)} %bitcast.50, f32[512,128]{1,0:T(8,128)} %bitcast.55, f32[64,128]{1,0:T(8,128)} %lookup.2.refs_4_, f32[64,128]{1,0:T(8,128)} %lookup.3.refs_5_, ...), custom_call_target="tpu_custom_call" | custom-call | flops 1600000000 | bytes 1048576 | tf_op jit(solution)/shard_map/star/pallas_call | solution.py:287
  98.8 9.7 %all-to-all-start.2 = ((f32[128,4,128]{2,1,0:T(4,128)}), f32[128,4,128]{2,1,0:T(4,128)S(1)}, u32[]{:S(2)}, u32[]{:S(2)}) async-start(f32[128,4,128]{2,1,0:T(4,128)} %bitcast.58), calls=%async_computation.2 | async-start | bytes 524288 | tf_op jit(solution)/shard_map/all_to_all | solution.py:209
  108.5 20.8 %spread.2.refs_4_ = f32[8512,128]{1,0:T(8,128)} custom-call(s32[128,128]{1,0:T(8,128)} %get-tuple-element.25.refs_0_, s32[128,128]{1,0:T(8,128)} %get-tuple-element.24.refs_2_.refs_1_, f32[128,128]{1,0:T(8,128)} %get-tuple-element.16.refs_2_, f32[128,128]{1,0:T(8,128)} %get-tuple-element.17.refs_3_), custom_call_target="tpu_custom_call" | custom-call | flops 4000000000 | bytes 5242880 | tf_op jit(solution)/shard_map/spread/pallas_call | solution.py:365
  129.3 0.0 all-to-all-done.2
  129.3 0.0 copy-start.3
  129.3 0.7 copy-done.3
  130.0 1.7 scan.3
  131.7 9.8 %all-to-all-start.3 = ((f32[128,2,128]{2,1,0:T(2,128)}), f32[128,2,128]{2,1,0:T(2,128)S(1)}, u32[]{:S(2)}, u32[]{:S(2)}) async-start(f32[128,2,128]{2,1,0:T(2,128)} %bitcast.59), calls=%async_computation.3 | async-start | bytes 262144 | tf_op jit(solution)/shard_map/all_to_all | solution.py:209
  141.5 21.7 %spread.3.refs_2_ = f32[8512,128]{1,0:T(8,128)} custom-call(s32[128,128]{1,0:T(8,128)} %get-tuple-element.25.refs_0_, s32[128,128]{1,0:T(8,128)} %get-tuple-element.24.refs_2_.refs_1_, f32[128,128]{1,0:T(8,128)} %get-tuple-element.16.refs_2_, f32[128,128]{1,0:T(8,128)} %get-tuple-element.17.refs_3_, f32[8512,128]{1,0:T(8,128)} %spread.2.refs_4_), custom_call_target="tpu_custom_call" | custom-call | flops 4000000000 | bytes 5242880 | tf_op jit(solution)/shard_map/spread/pallas_call | solution.py:365
  163.2 4.5 %extinction.1 = f32[4,2048,128]{2,1,0:T(8,128)} custom-call(f32[256,128]{1,0:T(8,128)} %bitcast.51, f32[8512,128]{1,0:T(8,128)} %get-tuple-element.12.refs_1_), custom_call_target="tpu_custom_call" | custom-call | flops 800000000 | bytes 8388608 | tf_op jit(solution)/shard_map/extinction/pallas_call | solution.py:421
  167.7 0.0 all-to-all-done.3
  167.7 0.6 copy-done.1
  168.3 6.4 %sensitivity.1 = f32[4,2048,128]{2,1,0:T(8,128)} custom-call(f32[256,128]{1,0:T(8,128)} %bitcast.52, f32[8192,128]{1,0:T(8,128)} %get-tuple-element.15.refs_1_, f32[8512,128]{1,0:T(8,128)} %spread.3.refs_2_), custom_call_target="tpu_custom_call" | custom-call | flops 1000000000 | bytes 12582912 | tf_op jit(solution)/shard_map/sensitivity/pallas_call | solution.py:471
  (5 shorter events, 0.0 us)
Async XLA Ops:
  2.4 14.7 %collective-permute-start.1 = (f32[256,4,128]{2,1,0:T(4,128)S(1)}, f32[256,4,128]{2,1,0:T(4,128)S(1)}, u32[]{:S(2)}, u32[]{:S(2)}) collective-permute-start(f32[256,4,128]{2,1,0:T(4,128)S(1)} %get-tuple-element.22), channel_id=1, source_target_pairs={{2,0},{4,2},{6,4},{8,6},{10,8},{12,10},{14,12},{16,14},{18,16},{20... | collective-permute-start | bytes 1572872 | tf_op jit(solution)/shard_map/ppermute | solution.py:521
  4.3 14.6 %collective-permute-start = (f32[256,4,128]{2,1,0:T(4,128)S(1)}, f32[256,4,128]{2,1,0:T(4,128)S(1)}, u32[]{:S(2)}, u32[]{:S(2)}) collective-permute-start(f32[256,4,128]{2,1,0:T(4,128)S(1)} %get-tuple-element.23), channel_id=1, source_target_pairs={{0,2},{2,4},{4,6},{6,8},{8,10},{10,12},{12,14},{14,16},{16,18},{18... | collective-permute-start | bytes 1572872 | tf_op jit(solution)/shard_map/ppermute | solution.py:520
  17.1 1.8 %copy-start.4 = (f32[256,4,128]{2,1,0:T(4,128)}, f32[256,4,128]{2,1,0:T(4,128)S(1)}, u32[]{:S(2)}) copy-start(f32[256,4,128]{2,1,0:T(4,128)S(1)} %collective-permute-done.1) | copy-start | bytes 1572868
  18.9 0.8 copy-start.5
  26.6 29.9 %all-to-all-start = ((f32[128,4,128]{2,1,0:T(4,128)}), f32[128,4,128]{2,1,0:T(4,128)S(1)}, u32[]{:S(2)}, u32[]{:S(2)}) async-start(f32[128,4,128]{2,1,0:T(4,128)} %bitcast.57), calls=%async_computation | async-start | bytes 524288 | tf_op jit(solution)/shard_map/all_to_all | solution.py:209
  56.5 0.7 copy-start.2
  58.9 24.3 %all-to-all-start.1 = ((f32[128,2,128]{2,1,0:T(2,128)}), f32[128,2,128]{2,1,0:T(2,128)S(1)}, u32[]{:S(2)}, u32[]{:S(2)}) async-start(f32[128,2,128]{2,1,0:T(2,128)} %bitcast.60), calls=%async_computation.1 | async-start | bytes 262144 | tf_op jit(solution)/shard_map/all_to_all | solution.py:209
  83.2 0.6 copy-start
  98.8 30.5 %all-to-all-start.2 = ((f32[128,4,128]{2,1,0:T(4,128)}), f32[128,4,128]{2,1,0:T(4,128)S(1)}, u32[]{:S(2)}, u32[]{:S(2)}) async-start(f32[128,4,128]{2,1,0:T(4,128)} %bitcast.58), calls=%async_computation.2 | async-start | bytes 524288 | tf_op jit(solution)/shard_map/all_to_all | solution.py:209
  129.3 0.7 copy-start.3
  131.7 36.0 %all-to-all-start.3 = ((f32[128,2,128]{2,1,0:T(2,128)}), f32[128,2,128]{2,1,0:T(2,128)S(1)}, u32[]{:S(2)}, u32[]{:S(2)}) async-start(f32[128,2,128]{2,1,0:T(2,128)} %bitcast.59), calls=%async_computation.3 | async-start | bytes 262144 | tf_op jit(solution)/shard_map/all_to_all | solution.py:209
  167.7 0.6 copy-start.1

commit v3 on v2

--- a/solution.py
+++ b/solution.py
@@ -9,7 +9,10 @@
 LANES = 128
 SUB = 8
 LEAD = 8
-ACCS = 4
+ACCS = 5
+TEAM = 4
+PAIR = 2
+STEP = 32
 CHUNKS = 8
 SPLIT = 7
 PACK = 64
@@ -146,7 +149,17 @@
     )(edge, obs, inv, exc, up, down)
 
 
-def lookup_kernel(first, idx_ref, tab_ref, low_ref, frac_ref, out_ref):
+def team_sizes(team, first, count_ref, work):
+    steps = lax.div(count_ref[1, first] + (STEP - 1), STEP)
+    for size in range(1, LANES // STEP + 1):
+        @pl.when(steps == size)
+        def _(size=size):
+            work([count_ref[0, first + t] for t in range(team)], size * STEP)
+
+
+def lookup_kernel(part, parts, chained, count_ref, idx_ref, tab_ref, low_ref, frac_ref, *refs):
+    out_ref = refs[-1]
+    out_ref[...] = refs[0][...] if chained else jnp.zeros_like(out_ref)
     lane = lax.broadcasted_iota(jnp.int32, (SUB, LANES), 1)
     sub = lax.broadcasted_iota(jnp.int32, (SUB, LANES), 0)
     pair = [(sub >> 1) == j for j in range(4)]
@@ -154,31 +167,40 @@
     is_inner = sub == (lane & 3) * 2
     is_outer = sub == (lane & 3) * 2 + 1
 
-    def body(o, carry):
-        low = jnp.broadcast_to(low_ref[pl.ds(o + first, 1), :], (SUB, LANES))
-        got = jnp.zeros((SUB, LANES), jnp.float32)
-        for k in range(LANES // 4):
-            rows = tab_ref[pl.ds(idx_ref[o + first, 4 * k], SUB), :]
-            for j in range(1, 4):
-                rows = jnp.where(pair[j], tab_ref[pl.ds(idx_ref[o + first, 4 * k + j] - 2 * j, SUB), :], rows)
-            got = jnp.where(quad == k, jnp.take_along_axis(rows, low, axis=1), got)
-        inner = jnp.sum(jnp.where(is_inner, got, 0.0), axis=0, keepdims=True)
-        outer = jnp.sum(jnp.where(is_outer, got, 0.0), axis=0, keepdims=True)
-        out_ref[pl.ds(o, 1), :] = inner + frac_ref[pl.ds(o + first, 1), :] * (outer - inner)
+    def work(owners, slots):
+        low = [jnp.broadcast_to(low_ref[pl.ds(o, 1), :], (SUB, LANES)) for o in owners]
+        at = [idx_ref.at[o] for o in owners]
+        got = [jnp.zeros((SUB, LANES), jnp.float32) for _ in owners]
+        for k in range(slots // 4):
+            rows = [None] * len(owners)
+            for j in range(4):
+                for t in range(len(owners)):
+                    value = tab_ref[pl.ds(at[t][4 * k + j] - 2 * j, SUB), :]
+                    rows[t] = value if j == 0 else jnp.where(pair[j], value, rows[t])
+            for t in range(len(owners)):
+                got[t] = jnp.where(quad == k, jnp.take_along_axis(rows[t], low[t], axis=1), got[t])
+        for t, o in enumerate(owners):
+            inner = jnp.sum(jnp.where(is_inner, got[t], 0.0), axis=0, keepdims=True)
+            outer = jnp.sum(jnp.where(is_outer, got[t], 0.0), axis=0, keepdims=True)
+            out_ref[pl.ds(o, 1), :] = inner + frac_ref[pl.ds(o, 1), :] * (outer - inner)
+
+    def body(i, carry):
+        team_sizes(TEAM, (i * parts + part) * TEAM, count_ref, work)
         return carry
 
-    lax.fori_loop(0, out_ref.shape[0], body, 0)
-
-
-def lookup_call(idx, tab, low, frac, first, count):
-    return pl.pallas_call(
-        lambda *refs: lookup_kernel(first, *refs),
-        out_shape=jax.ShapeDtypeStruct((count, LANES), jnp.float32),
-        in_specs=[SMEM, VMEM, VMEM, VMEM],
+    lax.fori_loop(0, out_ref.shape[0] // (TEAM * parts), body, 0)
+
+
+def lookup_call(counts, idx, tab, low, frac, part, parts, column=None):
+    extra = () if column is None else (column,)
+    return pl.pallas_call(
+        lambda *refs: lookup_kernel(part, parts, column is not None, *refs),
+        out_shape=jax.ShapeDtypeStruct(low.shape, jnp.float32),
+        in_specs=[SMEM, SMEM] + [VMEM] * (3 + len(extra)),
         out_specs=VMEM,
-        cost_estimate=cost(15, 5 << 20),
+        cost_estimate=cost(12, 5 << 20),
         name="lookup",
-    )(idx, tab, low, frac)
+    )(counts, idx, tab, low, frac, *extra)
 
 
 def scan_kernel(reverse, in_ref, out_ref, *field_ref):
@@ -215,7 +237,7 @@
     return high, (x - high.astype(jnp.float32)).astype(jnp.bfloat16)
 
 
-def star_kernel(devices, count_ref, pix_ref, off_ref, held_ref, col_a_ref, col_b_ref, frac_ref,
+def star_kernel(devices, count_ref, pix_ref, off_ref, held_ref, col_ref, frac_ref,
                 pay_ref, here_ref, inner_ref, acc_ref, tail_ref):
     groups = off_ref.shape[0]
     rows = SUB
@@ -230,9 +252,8 @@
     acc_ref[...] = jnp.zeros_like(acc_ref)
     pay_ref[pl.ds(1, devices, stride=FIELDS), :] = jnp.zeros((devices, LANES), jnp.float32)
 
-    def body(b, col_ref, shift):
+    def body(b):
         at = pl.ds(pl.multiple_of(b * rows, rows), rows)
-        local = pl.ds(pl.multiple_of((b - shift) * rows, rows), rows)
         pix = pix_ref[at, :]
         high = lax.shift_right_logical(pix, 7)
         high = (lax.rem(high, devices)) * (groups // devices) + lax.div(high, devices)
@@ -246,13 +267,13 @@
             part = found[:, j * LANES:(j + 1) * LANES]
             part = jnp.where(lanes[j], part[:LANES] + part[LANES:], 0.0)
             off_at.append(jnp.sum(part, axis=0, keepdims=True))
-        column = col_ref[local, :] + jnp.concatenate(off_at, axis=0)
-        transmit = jnp.exp(-column)
+        column = col_ref[at, :] + jnp.concatenate(off_at, axis=0)
         obs = held_ref[pl.ds(b * rows * FIELDS, rows, stride=FIELDS), :]
         inv = held_ref[pl.ds(b * rows * FIELDS + 1, rows, stride=FIELDS), :]
         live = jnp.zeros((rows, LANES), jnp.int32)
         for j in range(rows):
             live = jnp.where(sub == j, count_ref[0, b * rows + j], live)
+        transmit = jnp.exp(-jnp.where(slot < live, column, 0.0))
         residual = jnp.where(slot < live, (obs - (1.0 - transmit)) * inv, 0.0)
         pull = -residual * inv * transmit
         inner = (1.0 - frac_ref[at, :]) * pull
@@ -266,79 +287,73 @@
         acc_ref[...] += lax.dot_general(
             pick, spread, (((1,), (1,)), ((), ())), preferred_element_type=jnp.float32)
 
-    half = col_a_ref.shape[0] // rows
-    full = pix_ref.shape[0] // rows
-
-    @pl.loop(0, half)
+    @pl.loop(0, pix_ref.shape[0] // (2 * rows))
     def _(b):
-        body(b, col_a_ref, 0)
-
-    @pl.loop(half, full)
-    def _(b):
-        body(b, col_b_ref, half)
+        body(2 * b)
+        body(2 * b + 1)
 
     tail_ref[...] = acc_ref[:, :LANES] + acc_ref[:, LANES:]
     for e in range(groups // devices):
         pay_ref[pl.ds(2 + e, devices, stride=FIELDS), :] = tail_ref[pl.ds(e, devices, stride=groups // devices), :]
 
 
-def star_call(count, pix, off, held, col_a, col_b, frac, devices):
+def star_call(count, pix, off, held, column, frac, devices):
     slots = jax.ShapeDtypeStruct(pix.shape, jnp.float32)
     return pl.pallas_call(
         lambda *refs: star_kernel(devices, *refs),
         out_shape=[jax.ShapeDtypeStruct(held.shape, jnp.float32), slots, slots],
-        in_specs=[SMEM] + [VMEM] * 6,
+        in_specs=[SMEM] + [VMEM] * 5,
         out_specs=[VMEM] * 3,
         scratch_shapes=[pltpu.VMEM((off.shape[0], 2 * LANES), jnp.float32), pltpu.VMEM(off.shape, jnp.float32)],
         cost_estimate=cost(8, 1 << 20),
         name="star",
-    )(count, pix, off, held, col_a, col_b, frac)
-
-
-def spread_kernel(first, count, start, idx_ref, low_ref, here_ref, inner_ref, *refs):
-    if start:
-        start_hbm, refs = refs[0], refs[1:]
-    out_hbm = refs[0]
-    accs = refs[1:1 + ACCS]
-    sem = refs[1 + ACCS]
+    )(count, pix, off, held, column, frac)
+
+
+def spread_kernel(count_ref, idx_ref, low_ref, here_ref, inner_ref, out_hbm, *refs):
+    accs = refs[:ACCS]
+    sem = refs[ACCS]
     total_rows = out_hbm.shape[0]
     piece = total_rows // SPLIT
 
-    if start:
-        begin = pltpu.make_async_copy(start_hbm, accs[0], sem.at[SPLIT])
-        begin.start()
-
     def clear(i, carry):
-        for acc in accs[1 if start else 0:]:
+        for acc in accs:
             acc[pl.ds(pl.multiple_of(i * PACK, PACK), PACK), :] = jnp.zeros((PACK, LANES), jnp.float32)
         return carry
 
     lax.fori_loop(0, total_rows // PACK, clear, 0)
-    if start:
-        begin.wait()
     lane = lax.broadcasted_iota(jnp.int32, (SUB, LANES), 1)
     sub = lax.broadcasted_iota(jnp.int32, (SUB, LANES), 0)
     pair = sub >> 1
     in_pair = [pair == j for j in range(4)]
     even = (sub & 1) == 0
 
-    def body(o, carry):
-        def row_of(ref):
+    def work(owners, slots):
+        def row_of(ref, o):
             return jnp.broadcast_to(ref[pl.ds(o, 1), :], (SUB, LANES))
 
-        low = row_of(low_ref)
-        value = jnp.where(even, row_of(inner_ref), row_of(here_ref))
-        for k in range(LANES // 4):
-            at = pair + 4 * k
-            here = jnp.take_along_axis(low, at, axis=1) == lane
-            four = jnp.where(here, jnp.take_along_axis(value, at, axis=1), 0.0)
+        low = [row_of(low_ref, o) for o in owners]
+        value = [jnp.where(even, row_of(inner_ref, o), row_of(here_ref, o)) for o in owners]
+        at = [idx_ref.at[o] for o in owners]
+        turn = 0
+        for k in range(slots // 4):
+            pick = pair + 4 * k
+            four = []
+            for t in range(len(owners)):
+                here = jnp.take_along_axis(low[t], pick, axis=1) == lane
+                four.append(jnp.where(here, jnp.take_along_axis(value[t], pick, axis=1), 0.0))
             for j in range(4):
-                acc = accs[(4 * k + j) % ACCS]
-                rows = pl.ds(idx_ref[o, 4 * k + j] - 2 * j, SUB)
-                acc[rows, :] = acc[rows, :] + jnp.where(in_pair[j], four, 0.0)
+                for t in range(len(owners)):
+                    acc = accs[turn % ACCS]
+                    turn += 1
+                    rows = pl.ds(at[t][4 * k + j] - 2 * j, SUB)
+                    acc[rows, :] = acc[rows, :] + jnp.where(in_pair[j], four[t], 0.0)
+
+    def body(i, carry):
+        team_sizes(PAIR, i * PAIR, count_ref, work)
         return carry
 
-    lax.fori_loop(first, first + count, body, 0)
+    lax.fori_loop(0, idx_ref.shape[0] // PAIR, body, 0)
 
     copies = []
     for i in range(SPLIT):
@@ -359,18 +374,17 @@
         copy.wait()
 
 
-def spread_call(idx, low, here, inner, rows, first, count, start=None):
+def spread_call(counts, idx, low, here, inner, rows):
     shape = (rows, LANES)
-    extra = () if start is None else (start,)
-    return pl.pallas_call(
-        lambda *refs: spread_kernel(first, count, start is not None, *refs),
+    return pl.pallas_call(
+        spread_kernel,
         out_shape=jax.ShapeDtypeStruct(shape, jnp.float32),
-        in_specs=[SMEM, VMEM, VMEM, VMEM] + [ANY] * len(extra),
+        in_specs=[SMEM, SMEM, VMEM, VMEM, VMEM],
         out_specs=ANY,
-        scratch_shapes=[pltpu.VMEM(shape, jnp.float32)] * ACCS + [pltpu.SemaphoreType.DMA((SPLIT + 1,))],
-        cost_estimate=cost(20, 5 << 20),
+        scratch_shapes=[pltpu.VMEM(shape, jnp.float32)] * ACCS + [pltpu.SemaphoreType.DMA((SPLIT,))],
+        cost_estimate=cost(30, 5 << 20),
         name="spread",
-    )(idx, low, here, inner, *extra)
+    )(counts, idx, low, here, inner)
 
 
 def chunked(work, inputs, outputs):
@@ -505,6 +519,16 @@
     return part
 
 
+def sorted_owners(count):
+    n = count.shape[0]
+    a = lax.broadcasted_iota(jnp.int32, (n, n), 0)
+    b = lax.broadcasted_iota(jnp.int32, (n, n), 1)
+    ahead = (count[None, :] > count[:, None]) | ((count[None, :] == count[:, None]) & (b < a))
+    place = jnp.sum(ahead.astype(jnp.int32), axis=1)
+    mine = place[None, :] == a
+    return jnp.stack((jnp.sum(jnp.where(mine, b, 0), axis=1), jnp.sum(jnp.where(mine, count[None, :], 0), axis=1)))
+
+
 def body(excitation, star_shell, star_pixel, star_fraction, star_count, observed, inverse_error):
     shells, pixels = excitation.shape
     blocks = lax.axis_size("shell")
@@ -513,7 +537,6 @@
     thickness = depth_span / (shells * blocks)
     groups = pixels // LANES
     tall = shells + 1
-    owners = star_shell.shape[1]
 
     up = [(i, i + 1) for i in range(blocks - 1)]
     down = [(i + 1, i) for i in range(blocks - 1)]
@@ -523,6 +546,7 @@
     pixel, fraction = star_pixel[0], star_fraction[0]
     low = pixel & (LANES - 1)
     idx = (pixel >> 7) * tall + star_shell[0] + LEAD
+    counts = sorted_owners(star_count[0])
     edge = jnp.stack(((me == 0).astype(jnp.float32), (me == blocks - 1).astype(jnp.float32)))
     dens, tab, parts = density_call(
         to_tiles(excitation),
@@ -532,18 +556,17 @@
 
     held = exchange(parts, devices)
     offset = exchange(scan_call(held, devices, False, False)[0], devices)
-    half = owners // 2
-    col_a = lookup_call(idx, tab, low, fraction, 0, half)
-    col_b = lookup_call(idx, tab, low, fraction, half, owners - half)
-
-    parts, here, inner = star_call(star_count, pixel, offset, held, col_a, col_b, fraction, devices)
-    sums, residual = scan_call(exchange(parts, devices), devices, True, True)
+    column = lookup_call(counts, idx, tab, low, fraction, 0, 2)
+    column = lookup_call(counts, idx, tab, low, fraction, 1, 2, column)
+
+    parts, here, inner = star_call(star_count, pixel, offset, held, column, fraction, devices)
+    extinction = extinction_call(tab, offset, shells, devices)
+    parts, extinction = lax.optimization_barrier((exchange(parts, devices), extinction))
+    sums, residual = scan_call(parts, devices, True, True)
     tail_offset = exchange(sums, devices)
 
     rows = table_rows(groups, tall)
-    drop = spread_call(idx, low, here, inner, rows, 0, half)
-    drop = spread_call(idx, low, here, inner, rows, half, owners - half, drop)
-    extinction = extinction_call(tab, offset, shells, devices)
+    drop = spread_call(counts, idx, low, here, inner, rows)
     sensitivity = sensitivity_call(dens, drop, tail_offset, shells, devices)
     return from_tiles(extinction), from_tiles(sensitivity), residual[:, None, :]
 

time: 177 us -> 153 us (0.86)
  Pallas kernels: 108 us -> 83.8 us
  other arithmetic: 2.14 us -> 4.44 us
    pallas_call x4 -> x3, Pallas kernels: 71.5 us -> 49.3 us  [the longest x1 27.5 us: spread_call(): pl.pallas_call(spread_kernel, out_shape=jax.ShapeDtypeStruct(shape, jnp.f...]
  transfers between devices with their start and end apart: 6 -> 6, of which waited for: 2 -> 3; matrix products, arithmetic and copies ran while one was open for 1% -> 3% of each run, Pallas kernels for 44% -> 35%
where the time goes in v3:
time: 153 us; the launch traced here: 152 us
  Pallas kernels  83.8 us (55%)
  starting transfers between devices  49.4 us (32%)
  waiting for transfers between devices  8.03 us (5%)
  local copies, waits for them, and re-layouts  5.21 us (3%)
  other arithmetic  4.44 us (3%)
    all_to_all x4, starting transfers between devices, exchange(): parts = lax.all_to_all(parts, BOTH, split_axis=0, concat_axis=0, tiled=True)  44.1 us
    pallas_call x1, Pallas kernels, spread_call(): pl.pallas_call(spread_kernel, out_shape=jax.ShapeDtypeStruct(shape, jnp.f...  27.5 us
    pallas_call x2, Pallas kernels, lookup_call(): pl.pallas_call(lambda *refs: lookup_kernel(part, parts, column is not Non...  21.8 us
    pallas_call x1, Pallas kernels, star_call(): pl.pallas_call(lambda *refs: star_kernel(devices, *refs), out_shape=[jax....  13.4 us
    pallas_call x1, Pallas kernels, density_call(): pl.pallas_call(lambda *refs: density_kernel(shells, groups, devices, thic...  6.96 us
    pallas_call x1, Pallas kernels, sensitivity_call(): pl.pallas_call(lambda *refs: sensitivity_kernel(shells, devices, *refs),...  6.37 us
    ppermute x1, waiting for transfers between devices, body(): lax.ppermute(edge_rows(excitation, slice(0, PASSES)), 'shell', down)  5.51 us
    pallas_call x1, Pallas kernels, extinction_call(): pl.pallas_call(lambda *refs: extinction_kernel(shells, devices, *refs), i...  4.48 us
  transfers between devices with their start and end apart: 6, of which 3 were waited for; matrix products, arithmetic and copies ran while one was open for 3% of the time, Pallas kernels for 35%

profile of v3, /device:TPU:87, one launch (start us, length us, event | category | flops | bytes accessed | tf_op | source)
XLA Modules:
  0.0 151.6 jit_solution(2709143872848805279)
XLA Ops:
  0.6 1.7 %slice_bitcast_fusion = (f32[256,4,128]{2,1,0:T(4,128)S(1)}, f32[256,4,128]{2,1,0:T(4,128)S(1)}) fusion(f32[32,32768]{1,0:T(8,128)} %param.7), kind=kLoop, calls=%fused_computation | loop fusion | bytes 2097152 | tf_op jit(solution)/shard_map/transpose | solution.py:518
  2.4 1.9 %collective-permute-start.1 = (f32[256,4,128]{2,1,0:T(4,128)S(1)}, f32[256,4,128]{2,1,0:T(4,128)S(1)}, u32[]{:S(2)}, u32[]{:S(2)}) collective-permute-start(f32[256,4,128]{2,1,0:T(4,128)S(1)} %get-tuple-element.31), channel_id=1, source_target_pairs={{2,0},{4,2},{6,4},{8,6},{10,8},{12,10},{14,12},{16,14},{18,16},{20... | collective-permute-start | bytes 1572872 | tf_op jit(solution)/shard_map/ppermute | solution.py:544
  4.3 3.4 %collective-permute-start = (f32[256,4,128]{2,1,0:T(4,128)S(1)}, f32[256,4,128]{2,1,0:T(4,128)S(1)}, u32[]{:S(2)}, u32[]{:S(2)}) collective-permute-start(f32[256,4,128]{2,1,0:T(4,128)S(1)} %get-tuple-element.32), channel_id=1, source_target_pairs={{0,2},{2,4},{4,6},{6,8},{8,10},{10,12},{12,14},{14,16},{16,18},{18... | collective-permute-start | bytes 1572872 | tf_op jit(solution)/shard_map/ppermute | solution.py:543
  7.7 0.7 add_convert_fusion.refs_0_
  8.3 0.9 convert_reduce_fusion
  9.2 0.8 select_reduce_fusion.1
  10.0 1.5 %broadcast_and_fusion = (s32[128,128]{1,0:T(8,128)}, s32[128,128]{1,0:T(8,128)}) fusion(s32[1,128,128]{2,1,0:T(8,128)} %param.9, s32[1,128,128]{2,1,0:T(8,128)} %param.8), kind=kLoop, calls=%fused_computation.11 | loop fusion | flops 81920 | bytes 262144 | tf_op jit(solution)/shard_map/and | solution.py:547
  11.5 5.5 %collective-permute-done.1 = f32[256,4,128]{2,1,0:T(4,128)S(1)} collective-permute-done((f32[256,4,128]{2,1,0:T(4,128)S(1)}, f32[256,4,128]{2,1,0:T(4,128)S(1)}, u32[]{:S(2)}, u32[]{:S(2)}) %collective-permute-start.1) | collective-permute-done | bytes 524320 | tf_op jit(solution)/shard_map/ppermute | solution.py:544
  17.1 1.8 %collective-permute-done = f32[256,4,128]{2,1,0:T(4,128)S(1)} collective-permute-done((f32[256,4,128]{2,1,0:T(4,128)S(1)}, f32[256,4,128]{2,1,0:T(4,128)S(1)}, u32[]{:S(2)}, u32[]{:S(2)}) %collective-permute-start) | collective-permute-done | bytes 524320 | tf_op jit(solution)/shard_map/ppermute | solution.py:543
  18.9 0.8 copy-done.5
  19.7 7.0 %density.1 = (f32[8192,128]{1,0:T(8,128)}, f32[8512,128]{1,0:T(8,128)}, f32[512,128]{1,0:T(8,128)}) custom-call(f32[2]{0:T(128)} %add_convert_fusion.refs_0_, f32[128,128]{1,0:T(8,128)} %bitcast.71, f32[128,128]{1,0:T(8,128)} %bitcast.72, f32[4,2048,128]{2,1,0:T(8,128)} %bitcast.56, f32[1024,128]{1,0:T(8,128)} %bitcast.70, f32[1024,128]{1,0:T(8,128)} %bitcast.69), custom_call_target="tpu_custom_call" | custom-call | flops 1600000000 | bytes 12582912 | tf_op jit(solution)/shard_map/density/pallas_call | solution.py:129
  26.7 15.4 %all-to-all-start = ((f32[128,4,128]{2,1,0:T(4,128)}), f32[128,4,128]{2,1,0:T(4,128)S(1)}, u32[]{:S(2)}, u32[]{:S(2)}) async-start(f32[128,4,128]{2,1,0:T(4,128)} %bitcast.59), calls=%async_computation | async-start | bytes 524288 | tf_op jit(solution)/shard_map/all_to_all | solution.py:231
  42.0 0.6 pad_add_fusion.refs_0_.count_ref
  42.6 10.9 %lookup.2.refs_5_ = f32[128,128]{1,0:T(8,128)} custom-call(s32[2,128]{1,0:T(2,128)} %pad_add_fusion.refs_0_.count_ref, s32[128,128]{1,0:T(8,128)} %get-tuple-element.34.refs_1_.idx_ref, f32[8512,128]{1,0:T(8,128)} %get-tuple-element.14.refs_2_.refs_1_, s32[128,128]{1,0:T(8,128)} %get-tuple-element.33.refs_3_.low_ref, f32[128,128]{1,0:T(8,128)} %bitcast.73), custom_call_target="tpu_custom_call" | custom-call | flops 2400000000 | bytes 5242880 | tf_op jit(solution)/shard_map/lookup/pallas_call | solution.py:196
  53.5 0.0 all-to-all-done
  53.5 0.7 copy-done.2
  54.2 1.7 %scan.2 = f32[256,128]{1,0:T(8,128)} custom-call(f32[512,128]{1,0:T(8,128)} %bitcast.57), custom_call_target="tpu_custom_call" | custom-call | flops 200000000 | bytes 262144 | tf_op jit(solution)/shard_map/scan/pallas_call | solution.py:221
  55.9 9.2 %all-to-all-start.1 = ((f32[128,2,128]{2,1,0:T(2,128)}), f32[128,2,128]{2,1,0:T(2,128)S(1)}, u32[]{:S(2)}, u32[]{:S(2)}) async-start(f32[128,2,128]{2,1,0:T(2,128)} %bitcast.63), calls=%async_computation.1 | async-start | bytes 262144 | tf_op jit(solution)/shard_map/all_to_all | solution.py:231
  65.1 10.9 %lookup.3.refs_4_ = f32[128,128]{1,0:T(8,128)} custom-call(s32[2,128]{1,0:T(2,128)} %pad_add_fusion.refs_0_.count_ref, s32[128,128]{1,0:T(8,128)} %get-tuple-element.34.refs_1_.idx_ref, f32[8512,128]{1,0:T(8,128)} %get-tuple-element.14.refs_2_.refs_1_, s32[128,128]{1,0:T(8,128)} %get-tuple-element.33.refs_3_.low_ref, f32[128,128]{1,0:T(8,128)} %bitcast.74, ...), custom_call_target="tpu_custom_call" | custom-call | flops 2400000000 | bytes 5242880 | tf_op jit(solution)/shard_map/lookup/pallas_call | solution.py:196
  76.0 0.0 all-to-all-done.1
  76.0 0.7 copy-done
  76.7 13.4 %star.1 = (f32[512,128]{1,0:T(8,128)}, f32[128,128]{1,0:T(8,128)}, f32[128,128]{1,0:T(8,128)}) custom-call(s32[1,128]{1,0:T(1,128)} %refs_0_.1, s32[128,128]{1,0:T(8,128)} %bitcast.64, f32[256,128]{1,0:T(8,128)} %bitcast.53, f32[512,128]{1,0:T(8,128)} %bitcast.58, f32[128,128]{1,0:T(8,128)} %lookup.3.refs_4_, f32[128,128]{1,0:T(8,128)} %bitcast.75), custom_call_target="tpu_custom_call" | custom-call | flops 1600000000 | bytes 1048576 | tf_op jit(solution)/shard_map/star/pallas_call | solution.py:302
  90.0 9.2 %all-to-all-start.2 = ((f32[128,4,128]{2,1,0:T(4,128)}), f32[128,4,128]{2,1,0:T(4,128)S(1)}, u32[]{:S(2)}, u32[]{:S(2)}) async-start(f32[128,4,128]{2,1,0:T(4,128)} %bitcast.61), calls=%async_computation.2 | async-start | bytes 524288 | tf_op jit(solution)/shard_map/all_to_all | solution.py:231
  99.2 4.5 %extinction.1 = f32[4,2048,128]{2,1,0:T(8,128)} custom-call(f32[256,128]{1,0:T(8,128)} %bitcast.54, f32[8512,128]{1,0:T(8,128)} %get-tuple-element.14.refs_2_.refs_1_), custom_call_target="tpu_custom_call" | custom-call | flops 800000000 | bytes 8388608 | tf_op jit(solution)/shard_map/extinction/pallas_call | solution.py:435
  103.7 0.7 all-to-all-done.2
  104.4 0.7 copy-done.3
  105.1 1.7 %scan.3 = (f32[256,128]{1,0:T(8,128)}, f32[128,128]{1,0:T(8,128)}) custom-call(f32[512,128]{1,0:T(8,128)} %bitcast.60), custom_call_target="tpu_custom_call" | custom-call | flops 200000000 | bytes 262144 | tf_op jit(solution)/shard_map/scan/pallas_call | solution.py:221
  106.8 10.3 %all-to-all-start.3 = ((f32[128,2,128]{2,1,0:T(2,128)}), f32[128,2,128]{2,1,0:T(2,128)S(1)}, u32[]{:S(2)}, u32[]{:S(2)}) async-start(f32[128,2,128]{2,1,0:T(2,128)} %bitcast.62), calls=%async_computation.3 | async-start | bytes 262144 | tf_op jit(solution)/shard_map/all_to_all | solution.py:231
  117.1 27.5 %spread.1.refs_2_ = f32[8512,128]{1,0:T(8,128)} custom-call(s32[2,128]{1,0:T(2,128)} %pad_add_fusion.refs_0_.count_ref, s32[128,128]{1,0:T(8,128)} %get-tuple-element.34.refs_1_.idx_ref, s32[128,128]{1,0:T(8,128)} %get-tuple-element.33.refs_3_.low_ref, f32[128,128]{1,0:T(8,128)} %get-tuple-element.20.here_ref, f32[128,128]{1,0:T(8,128)} %get-tuple-element.21.inner_ref), custom_call_target="tpu_custom_call" | custom-call | flops 6000000000 | bytes 5242880 | tf_op jit(solution)/shard_map/spread/pallas_call | solution.py:379
  144.6 0.0 all-to-all-done.3
  144.6 0.6 copy-done.1
  145.2 6.4 %sensitivity.1 = f32[4,2048,128]{2,1,0:T(8,128)} custom-call(f32[256,128]{1,0:T(8,128)} %bitcast.55, f32[8192,128]{1,0:T(8,128)} %get-tuple-element.19.refs_1_, f32[8512,128]{1,0:T(8,128)} %spread.1.refs_2_), custom_call_target="tpu_custom_call" | custom-call | flops 1000000000 | bytes 12582912 | tf_op jit(solution)/shard_map/sensitivity/pallas_call | solution.py:485
  (7 shorter events, 0.0 us)
Async XLA Ops:
  2.4 14.7 %collective-permute-start.1 = (f32[256,4,128]{2,1,0:T(4,128)S(1)}, f32[256,4,128]{2,1,0:T(4,128)S(1)}, u32[]{:S(2)}, u32[]{:S(2)}) collective-permute-start(f32[256,4,128]{2,1,0:T(4,128)S(1)} %get-tuple-element.31), channel_id=1, source_target_pairs={{2,0},{4,2},{6,4},{8,6},{10,8},{12,10},{14,12},{16,14},{18,16},{20... | collective-permute-start | bytes 1572872 | tf_op jit(solution)/shard_map/ppermute | solution.py:544
  4.3 14.6 %collective-permute-start = (f32[256,4,128]{2,1,0:T(4,128)S(1)}, f32[256,4,128]{2,1,0:T(4,128)S(1)}, u32[]{:S(2)}, u32[]{:S(2)}) collective-permute-start(f32[256,4,128]{2,1,0:T(4,128)S(1)} %get-tuple-element.32), channel_id=1, source_target_pairs={{0,2},{2,4},{4,6},{6,8},{8,10},{10,12},{12,14},{14,16},{16,18},{18... | collective-permute-start | bytes 1572872 | tf_op jit(solution)/shard_map/ppermute | solution.py:543
  17.1 1.8 %copy-start.4 = (f32[256,4,128]{2,1,0:T(4,128)}, f32[256,4,128]{2,1,0:T(4,128)S(1)}, u32[]{:S(2)}) copy-start(f32[256,4,128]{2,1,0:T(4,128)S(1)} %collective-permute-done.1) | copy-start | bytes 1572868
  18.9 0.8 copy-start.5
  26.7 26.9 %all-to-all-start = ((f32[128,4,128]{2,1,0:T(4,128)}), f32[128,4,128]{2,1,0:T(4,128)S(1)}, u32[]{:S(2)}, u32[]{:S(2)}) async-start(f32[128,4,128]{2,1,0:T(4,128)} %bitcast.59), calls=%async_computation | async-start | bytes 524288 | tf_op jit(solution)/shard_map/all_to_all | solution.py:231
  53.5 0.7 copy-start.2
  55.9 20.1 %all-to-all-start.1 = ((f32[128,2,128]{2,1,0:T(2,128)}), f32[128,2,128]{2,1,0:T(2,128)S(1)}, u32[]{:S(2)}, u32[]{:S(2)}) async-start(f32[128,2,128]{2,1,0:T(2,128)} %bitcast.63), calls=%async_computation.1 | async-start | bytes 262144 | tf_op jit(solution)/shard_map/all_to_all | solution.py:231
  76.0 0.7 copy-start
  90.0 14.4 %all-to-all-start.2 = ((f32[128,4,128]{2,1,0:T(4,128)}), f32[128,4,128]{2,1,0:T(4,128)S(1)}, u32[]{:S(2)}, u32[]{:S(2)}) async-start(f32[128,4,128]{2,1,0:T(4,128)} %bitcast.61), calls=%async_computation.2 | async-start | bytes 524288 | tf_op jit(solution)/shard_map/all_to_all | solution.py:231
  104.4 0.7 copy-start.3
  106.8 37.8 %all-to-all-start.3 = ((f32[128,2,128]{2,1,0:T(2,128)}), f32[128,2,128]{2,1,0:T(2,128)S(1)}, u32[]{:S(2)}, u32[]{:S(2)}) async-start(f32[128,2,128]{2,1,0:T(2,128)} %bitcast.62), calls=%async_computation.3 | async-start | bytes 262144 | tf_op jit(solution)/shard_map/all_to_all | solution.py:231
  144.6 0.6 copy-start.1

commit v4 on v3

--- a/solution.py
+++ b/solution.py
@@ -1,3 +1,4 @@
+import math
 import jax
 import jax.numpy as jnp
 from jax import lax
@@ -9,7 +10,7 @@
 LANES = 128
 SUB = 8
 LEAD = 8
-ACCS = 5
+ACCS = 6
 TEAM = 4
 PAIR = 2
 STEP = 32
@@ -17,6 +18,7 @@
 SPLIT = 7
 PACK = 64
 FIELDS = 4
+LOG2E = math.log2(math.e)
 BOTH = ("shell", "sky")
 
 
@@ -55,7 +57,7 @@
                    dens_hbm, tab_hbm, pay_ref, exc_ref, up_ref, down_ref, dens_ref, tab_ref, in_sem, out_sem):
     tall = shells + 1
     per = groups // CHUNKS
-    weight = taps()
+    weight = [v * LOG2E for v in taps()]
     low_edge = edge_ref[0]
     high_edge = edge_ref[1]
 
@@ -100,7 +102,7 @@
             value = weight[0] * exc[r]
             for k in range(1, PASSES + 1):
                 value = value + weight[k] * (exc[r - k] + exc[r + k])
-            dens = jnp.exp(value)
+            dens = jnp.exp2(value)
             dens_ref[pl.ds((g * shells + r) * SUB, SUB), :] = dens
             step = dens * thickness
             total = step if total is None else total + step
@@ -149,17 +151,30 @@
     )(edge, obs, inv, exc, up, down)
 
 
-def team_sizes(team, first, count_ref, work):
-    steps = lax.div(count_ref[1, first] + (STEP - 1), STEP)
+def team_sizes(team, first, order_ref, count_ref, work):
+    steps = lax.div(count_ref[first] + (STEP - 1), STEP)
     for size in range(1, LANES // STEP + 1):
         @pl.when(steps == size)
         def _(size=size):
-            work([count_ref[0, first + t] for t in range(team)], size * STEP)
-
-
-def lookup_kernel(part, parts, chained, count_ref, idx_ref, tab_ref, low_ref, frac_ref, *refs):
-    out_ref = refs[-1]
-    out_ref[...] = refs[0][...] if chained else jnp.zeros_like(out_ref)
+            work([order_ref[first + t] for t in range(team)], size * STEP)
+
+
+def fetch(sources, targets, sem):
+    copies = [pltpu.make_async_copy(x, y, sem.at[i]) for i, (x, y) in enumerate(zip(sources, targets))]
+    for copy in copies:
+        copy.start()
+    return copies
+
+
+def lookup_kernel(part, parts, chained, order_ref, count_ref, *refs):
+    n = 5 if chained else 4
+    out_ref = refs[n]
+    sources, targets, sem = refs[:n], refs[n + 1:-1], refs[-1]
+    idx_ref, tab_ref, low_ref, frac_ref = targets
+    if not chained:
+        out_ref[...] = jnp.zeros_like(out_ref)
+    for copy in fetch(sources, targets + ((out_ref,) if chained else ()), sem):
+        copy.wait()
     lane = lax.broadcasted_iota(jnp.int32, (SUB, LANES), 1)
     sub = lax.broadcasted_iota(jnp.int32, (SUB, LANES), 0)
     pair = [(sub >> 1) == j for j in range(4)]
@@ -185,22 +200,29 @@
             out_ref[pl.ds(o, 1), :] = inner + frac_ref[pl.ds(o, 1), :] * (outer - inner)
 
     def body(i, carry):
-        team_sizes(TEAM, (i * parts + part) * TEAM, count_ref, work)
+        team_sizes(TEAM, (i * parts + part) * TEAM, order_ref, count_ref, work)
         return carry
 
     lax.fori_loop(0, out_ref.shape[0] // (TEAM * parts), body, 0)
 
 
-def lookup_call(counts, idx, tab, low, frac, part, parts, column=None):
+def lookup_call(order, counts, idx, tab, low, frac, part, parts, column=None):
     extra = () if column is None else (column,)
     return pl.pallas_call(
         lambda *refs: lookup_kernel(part, parts, column is not None, *refs),
         out_shape=jax.ShapeDtypeStruct(low.shape, jnp.float32),
-        in_specs=[SMEM, SMEM] + [VMEM] * (3 + len(extra)),
+        in_specs=[SMEM, SMEM] + [ANY] * (4 + len(extra)),
         out_specs=VMEM,
+        scratch_shapes=[
+            pltpu.SMEM(idx.shape, jnp.int32),
+            pltpu.VMEM(tab.shape, jnp.float32),
+            pltpu.VMEM(low.shape, jnp.int32),
+            pltpu.VMEM(frac.shape, jnp.float32),
+            pltpu.SemaphoreType.DMA((4 + len(extra),)),
+        ],
         cost_estimate=cost(12, 5 << 20),
         name="lookup",
-    )(counts, idx, tab, low, frac, *extra)
+    )(order, counts, idx, tab, low, frac, *extra)
 
 
 def scan_kernel(reverse, in_ref, out_ref, *field_ref):
@@ -222,6 +244,7 @@
         lambda *refs: scan_kernel(reverse, *refs),
         out_shape=shapes,
         cost_estimate=cost(1, 1 << 18),
+        compiler_params=pltpu.CompilerParams(vmem_limit_bytes=4 << 20),
         name="scan",
     )(parts)
 
@@ -240,9 +263,9 @@
 def star_kernel(devices, count_ref, pix_ref, off_ref, held_ref, col_ref, frac_ref,
                 pay_ref, here_ref, inner_ref, acc_ref, tail_ref):
     groups = off_ref.shape[0]
-    rows = SUB
+    rows = 2 * SUB
     offt = jnp.transpose(off_ref[...])
-    offt = jnp.concatenate(halves(offt), axis=0)
+    offt = jnp.concatenate(halves(offt), axis=1)
     group_id = lax.broadcasted_iota(jnp.int32, (groups, LANES), 0).astype(jnp.bfloat16)
     lane_id = lax.broadcasted_iota(jnp.int32, (LANES, LANES), 0)
     slot = lax.broadcasted_iota(jnp.int32, (rows, LANES), 1)
@@ -260,12 +283,12 @@
         high = high.astype(jnp.float32).astype(jnp.bfloat16)
         low = pix & 127
         pick = jnp.concatenate([jnp.where(group_id == high[j:j + 1, :], one, zero) for j in range(rows)], axis=1)
-        found = jnp.dot(offt, pick, preferred_element_type=jnp.float32)
+        found = jnp.dot(offt, jnp.concatenate((pick, pick), axis=0), preferred_element_type=jnp.float32)
         lanes = [lane_id == low[j:j + 1, :] for j in range(rows)]
         off_at = []
         for j in range(rows):
             part = found[:, j * LANES:(j + 1) * LANES]
-            part = jnp.where(lanes[j], part[:LANES] + part[LANES:], 0.0)
+            part = jnp.where(lanes[j], part, 0.0)
             off_at.append(jnp.sum(part, axis=0, keepdims=True))
         column = col_ref[at, :] + jnp.concatenate(off_at, axis=0)
         obs = held_ref[pl.ds(b * rows * FIELDS, rows, stride=FIELDS), :]
@@ -287,10 +310,9 @@
         acc_ref[...] += lax.dot_general(
             pick, spread, (((1,), (1,)), ((), ())), preferred_element_type=jnp.float32)
 
-    @pl.loop(0, pix_ref.shape[0] // (2 * rows))
+    @pl.loop(0, pix_ref.shape[0] // rows)
     def _(b):
-        body(2 * b)
-        body(2 * b + 1)
+        body(b)
 
     tail_ref[...] = acc_ref[:, :LANES] + acc_ref[:, LANES:]
     for e in range(groups // devices):
@@ -310,9 +332,12 @@
     )(count, pix, off, held, column, frac)
 
 
-def spread_kernel(count_ref, idx_ref, low_ref, here_ref, inner_ref, out_hbm, *refs):
-    accs = refs[:ACCS]
-    sem = refs[ACCS]
+def spread_kernel(order_ref, count_ref, *refs):
+    sources, out_hbm, targets = refs[:4], refs[4], refs[5:9]
+    accs = refs[9:9 + ACCS]
+    sem, in_sem = refs[9 + ACCS:]
+    idx_ref, low_ref, here_ref, inner_ref = targets
+    started = fetch(sources, targets, in_sem)
     total_rows = out_hbm.shape[0]
     piece = total_rows // SPLIT
 
@@ -322,6 +347,8 @@
         return carry
 
     lax.fori_loop(0, total_rows // PACK, clear, 0)
+    for copy in started:
+        copy.wait()
     lane = lax.broadcasted_iota(jnp.int32, (SUB, LANES), 1)
     sub = lax.broadcasted_iota(jnp.int32, (SUB, LANES), 0)
     pair = sub >> 1
@@ -350,7 +377,7 @@
                     acc[rows, :] = acc[rows, :] + jnp.where(in_pair[j], four[t], 0.0)
 
     def body(i, carry):
-        team_sizes(PAIR, i * PAIR, count_ref, work)
+        team_sizes(PAIR, i * PAIR, order_ref, count_ref, work)
         return carry
 
     lax.fori_loop(0, idx_ref.shape[0] // PAIR, body, 0)
@@ -374,17 +401,20 @@
         copy.wait()
 
 
-def spread_call(counts, idx, low, here, inner, rows):
+def spread_call(order, counts, idx, low, here, inner, rows):
     shape = (rows, LANES)
     return pl.pallas_call(
         spread_kernel,
         out_shape=jax.ShapeDtypeStruct(shape, jnp.float32),
-        in_specs=[SMEM, SMEM, VMEM, VMEM, VMEM],
+        in_specs=[SMEM, SMEM] + [ANY] * 4,
         out_specs=ANY,
-        scratch_shapes=[pltpu.VMEM(shape, jnp.float32)] * ACCS + [pltpu.SemaphoreType.DMA((SPLIT,))],
+        scratch_shapes=[pltpu.SMEM(idx.shape, jnp.int32), pltpu.VMEM(low.shape, jnp.int32)]
+        + [pltpu.VMEM(here.shape, jnp.float32)] * 2
+        + [pltpu.VMEM(shape, jnp.float32)] * ACCS
+        + [pltpu.SemaphoreType.DMA((SPLIT,)), pltpu.SemaphoreType.DMA((4,))],
         cost_estimate=cost(30, 5 << 20),
         name="spread",
-    )(counts, idx, low, here, inner)
+    )(order, counts, idx, low, here, inner)
 
 
 def chunked(work, inputs, outputs):
@@ -526,7 +556,7 @@
     ahead = (count[None, :] > count[:, None]) | ((count[None, :] == count[:, None]) & (b < a))
     place = jnp.sum(ahead.astype(jnp.int32), axis=1)
     mine = place[None, :] == a
-    return jnp.stack((jnp.sum(jnp.where(mine, b, 0), axis=1), jnp.sum(jnp.where(mine, count[None, :], 0), axis=1)))
+    return jnp.sum(jnp.where(mine, b, 0), axis=1), jnp.sum(jnp.where(mine, count[None, :], 0), axis=1)
 
 
 def body(excitation, star_shell, star_pixel, star_fraction, star_count, observed, inverse_error):
@@ -546,7 +576,9 @@
     pixel, fraction = star_pixel[0], star_fraction[0]
     low = pixel & (LANES - 1)
     idx = (pixel >> 7) * tall + star_shell[0] + LEAD
-    counts = sorted_owners(star_count[0])
+    order, counts = sorted_owners(star_count[0])
+    from_below, from_above, idx, low, order, counts = lax.optimization_barrier(
+        (from_below, from_above, idx, low, order, counts))
     edge = jnp.stack(((me == 0).astype(jnp.float32), (me == blocks - 1).astype(jnp.float32)))
     dens, tab, parts = density_call(
         to_tiles(excitation),
@@ -556,8 +588,8 @@
 
     held = exchange(parts, devices)
     offset = exchange(scan_call(held, devices, False, False)[0], devices)
-    column = lookup_call(counts, idx, tab, low, fraction, 0, 2)
-    column = lookup_call(counts, idx, tab, low, fraction, 1, 2, column)
+    column = lookup_call(order, counts, idx, tab, low, fraction, 0, 2)
+    column = lookup_call(order, counts, idx, tab, low, fraction, 1, 2, column)
 
     parts, here, inner = star_call(star_count, pixel, offset, held, column, fraction, devices)
     extinction = extinction_call(tab, offset, shells, devices)
@@ -566,7 +598,7 @@
     tail_offset = exchange(sums, devices)
 
     rows = table_rows(groups, tall)
-    drop = spread_call(counts, idx, low, here, inner, rows)
+    drop = spread_call(order, counts, idx, low, here, inner, rows)
     sensitivity = sensitivity_call(dens, drop, tail_offset, shells, devices)
     return from_tiles(extinction), from_tiles(sensitivity), residual[:, None, :]
 

time: 153 us -> 144 us (0.941)
  Pallas kernels: 83.8 us -> 73.4 us
  starting transfers between devices: 49.4 us -> 52.3 us
    pallas_call x1, Pallas kernels: 27.5 us -> 22.8 us  [spread_call(): pl.pallas_call(spread_kernel, out_shape=jax.ShapeDtypeStruct(shape, jnp.f...]
    pallas_call x1, Pallas kernels: 13.4 us -> 10.4 us  [star_call(): pl.pallas_call(lambda *refs: star_kernel(devices, *refs), out_shape=[jax....]
    all_to_all x4, starting transfers between devices: 44.1 us -> 47 us  [exchange(): parts = lax.all_to_all(parts, BOTH, split_axis=0, concat_axis=0, tiled=True)]
    pallas_call x2, Pallas kernels: 3.33 us -> 1.45 us  [scan_call(): pl.pallas_call(lambda *refs: scan_kernel(reverse, *refs), out_shape=shape...]
    and x1 -> x0, other arithmetic: 1.54 us -> none  [body(): low = pixel & LANES - 1]
    unnamed x12 -> x10, local copies, waits for them, and re-layouts: 3.48 us -> 2.09 us
  transfers between devices with their start and end apart: 6 -> 6, of which waited for: 3 -> 3; matrix products, arithmetic and copies ran while one was open for 3% -> 3% of each run, Pallas kernels for 35% -> 34%
where the time goes in v4:
time: 144 us; the launch traced here: 142 us
  Pallas kernels  73.4 us (51%)
  starting transfers between devices  52.3 us (36%)
  waiting for transfers between devices  8.25 us (6%)
  local copies, waits for them, and re-layouts  3.81 us (3%)
  other arithmetic  3.65 us (3%)
    all_to_all x4, starting transfers between devices, exchange(): parts = lax.all_to_all(parts, BOTH, split_axis=0, concat_axis=0, tiled=True)  47 us
    pallas_call x1, Pallas kernels, spread_call(): pl.pallas_call(spread_kernel, out_shape=jax.ShapeDtypeStruct(shape, jnp.f...  22.8 us
    pallas_call x2, Pallas kernels, lookup_call(): pl.pallas_call(lambda *refs: lookup_kernel(part, parts, column is not Non...  21 us
    pallas_call x1, Pallas kernels, star_call(): pl.pallas_call(lambda *refs: star_kernel(devices, *refs), out_shape=[jax....  10.4 us
    pallas_call x1, Pallas kernels, density_call(): pl.pallas_call(lambda *refs: density_kernel(shells, groups, devices, thic...  6.85 us
    pallas_call x1, Pallas kernels, sensitivity_call(): pl.pallas_call(lambda *refs: sensitivity_kernel(shells, devices, *refs),...  6.37 us
    ppermute x1, waiting for transfers between devices, body(): lax.ppermute(edge_rows(excitation, slice(0, PASSES)), 'shell', down)  5.74 us
    pallas_call x1, Pallas kernels, extinction_call(): pl.pallas_call(lambda *refs: extinction_kernel(shells, devices, *refs), i...  4.48 us
  transfers between devices with their start and end apart: 6, of which 3 were waited for; matrix products, arithmetic and copies ran while one was open for 3% of the time, Pallas kernels for 34%

profile of v4, /device:TPU:87, one launch (start us, length us, event | category | flops | bytes accessed | tf_op | source)
XLA Modules:
  0.0 142.2 jit_solution(8560835172318998309)
XLA Ops:
  0.6 1.7 %slice_bitcast_fusion = (f32[256,4,128]{2,1,0:T(4,128)S(1)}, f32[256,4,128]{2,1,0:T(4,128)S(1)}) fusion(f32[32,32768]{1,0:T(8,128)} %param.7), kind=kLoop, calls=%fused_computation | loop fusion | bytes 2097152 | tf_op jit(solution)/shard_map/transpose | solution.py:548
  2.4 1.9 %collective-permute-start.1 = (f32[256,4,128]{2,1,0:T(4,128)S(1)}, f32[256,4,128]{2,1,0:T(4,128)S(1)}, u32[]{:S(2)}, u32[]{:S(2)}) collective-permute-start(f32[256,4,128]{2,1,0:T(4,128)S(1)} %get-tuple-element.43), channel_id=1, source_target_pairs={{2,0},{4,2},{6,4},{8,6},{10,8},{12,10},{14,12},{16,14},{18,16},{20... | collective-permute-start | bytes 1572872 | tf_op jit(solution)/shard_map/ppermute | solution.py:574
  4.3 3.4 %collective-permute-start = (f32[256,4,128]{2,1,0:T(4,128)S(1)}, f32[256,4,128]{2,1,0:T(4,128)S(1)}, u32[]{:S(2)}, u32[]{:S(2)}) collective-permute-start(f32[256,4,128]{2,1,0:T(4,128)S(1)} %get-tuple-element.44), channel_id=1, source_target_pairs={{0,2},{2,4},{4,6},{6,8},{8,10},{10,12},{12,14},{14,16},{16,18},{18... | collective-permute-start | bytes 1572872 | tf_op jit(solution)/shard_map/ppermute | solution.py:573
  7.7 0.6 add_convert_fusion.refs_0_
  8.2 0.9 convert_reduce_fusion
  9.2 2.2 %select_reduce_fusion = (s32[128]{0:T(128)}, s32[128]{0:T(128)}, s32[128,128]{1,0:T(8,128)}, s32[128,128]{1,0:T(8,128)}) fusion(s32[128]{0:T(128)S(1)} %convert_reduce_fusion, s32[128]{0:T(128)} %bitcast.62, s32[1,128,128]{2,1,0:T(8,128)} %param.8, s32[1,128,128]{2,1,0:T(8,128)} %param.9), kind=kLoop, calls=%fused_computation.4 | loop fusion | flops 163584 | bytes 264192 | tf_op jit(solution)/shard_map/reduce_sum | solution.py:559
  11.3 5.7 %collective-permute-done.1 = f32[256,4,128]{2,1,0:T(4,128)S(1)} collective-permute-done((f32[256,4,128]{2,1,0:T(4,128)S(1)}, f32[256,4,128]{2,1,0:T(4,128)S(1)}, u32[]{:S(2)}, u32[]{:S(2)}) %collective-permute-start.1) | collective-permute-done | bytes 524320 | tf_op jit(solution)/shard_map/ppermute | solution.py:574
  17.1 1.8 %collective-permute-done = f32[256,4,128]{2,1,0:T(4,128)S(1)} collective-permute-done((f32[256,4,128]{2,1,0:T(4,128)S(1)}, f32[256,4,128]{2,1,0:T(4,128)S(1)}, u32[]{:S(2)}, u32[]{:S(2)}) %collective-permute-start) | collective-permute-done | bytes 524320 | tf_op jit(solution)/shard_map/ppermute | solution.py:573
  18.9 0.0 copy-done.3
  18.9 0.8 copy-done.4
  19.7 6.8 %density.1 = (f32[8192,128]{1,0:T(8,128)}, f32[8512,128]{1,0:T(8,128)}, f32[512,128]{1,0:T(8,128)}) custom-call(f32[2]{0:T(128)} %add_convert_fusion.refs_0_, f32[128,128]{1,0:T(8,128)} %bitcast.65, f32[128,128]{1,0:T(8,128)} %bitcast.66, f32[4,2048,128]{2,1,0:T(8,128)} %bitcast.57, f32[1024,128]{1,0:T(8,128)} %bitcast.64, f32[1024,128]{1,0:T(8,128)} %bitcast.63), custom_call_target="tpu_custom_call" | custom-call | flops 1600000000 | bytes 12582912 | tf_op jit(solution)/shard_map/density/pallas_call | solution.py:131
  26.5 15.4 %all-to-all-start = ((f32[128,4,128]{2,1,0:T(4,128)}), f32[128,4,128]{2,1,0:T(4,128)S(1)}, u32[]{:S(2)}, u32[]{:S(2)}) async-start(f32[128,4,128]{2,1,0:T(4,128)} %bitcast.59), calls=%async_computation | async-start | bytes 524288 | tf_op jit(solution)/shard_map/all_to_all | solution.py:254
  41.9 10.6 %lookup.2.refs_6_ = f32[128,128]{1,0:T(8,128)} custom-call(s32[128]{0:T(128)} %get-tuple-element.22.refs_0_.order_ref, s32[128]{0:T(128)} %get-tuple-element.23.refs_1_.count_ref, s32[128,128]{1,0:T(8,128)} %get-tuple-element.24.refs_2_.refs_0_, f32[8512,128]{1,0:T(8,128)} %get-tuple-element.25.refs_3_.refs_1_, ...), custom_call_target="tpu_custom_call" | custom-call | flops 2400000000 | bytes 5242880 | tf_op jit(solution)/shard_map/lookup/pallas_call | solution.py:211
  52.6 0.0 all-to-all-done
  52.6 0.0 copy-start
  52.6 0.7 scan.2
  53.3 10.6 %all-to-all-start.1 = ((f32[128,2,128]{2,1,0:T(2,128)}), f32[128,2,128]{2,1,0:T(2,128)S(1)}, u32[]{:S(2)}, u32[]{:S(2)}) async-start(f32[128,2,128]{2,1,0:T(2,128)} %bitcast.18), calls=%async_computation.1 | async-start | bytes 262144 | tf_op jit(solution)/shard_map/all_to_all | solution.py:254
  64.0 10.4 %lookup.3.refs_4_ = f32[128,128]{1,0:T(8,128)} custom-call(s32[128]{0:T(128)} %get-tuple-element.22.refs_0_.order_ref, s32[128]{0:T(128)} %get-tuple-element.23.refs_1_.count_ref, s32[128,128]{1,0:T(8,128)} %get-tuple-element.24.refs_2_.refs_0_, f32[8512,128]{1,0:T(8,128)} %get-tuple-element.25.refs_3_.refs_1_, ...), custom_call_target="tpu_custom_call" | custom-call | flops 2400000000 | bytes 5242880 | tf_op jit(solution)/shard_map/lookup/pallas_call | solution.py:211
  74.4 0.0 copy-done
  74.4 0.0 all-to-all-done.1
  74.4 0.0 copy-start.1
  74.4 0.6 copy-done.1
  75.0 10.4 %star.1 = (f32[512,128]{1,0:T(8,128)}, f32[128,128]{1,0:T(8,128)}, f32[128,128]{1,0:T(8,128)}) custom-call(s32[1,128]{1,0:T(1,128)} %refs_0_.1, s32[128,128]{1,0:T(8,128)} %bitcast.60, f32[256,128]{1,0:T(8,128)} %bitcast.54, f32[512,128]{1,0:T(8,128)} %bitcast.50, f32[128,128]{1,0:T(8,128)} %lookup.3.refs_4_, f32[128,128]{1,0:T(8,128)} %bitcast.69), custom_call_target="tpu_custom_call" | custom-call | flops 1600000000 | bytes 1048576 | tf_op jit(solution)/shard_map/star/pallas_call | solution.py:324
  85.5 10.6 %all-to-all-start.2 = ((f32[128,4,128]{2,1,0:T(4,128)}), f32[128,4,128]{2,1,0:T(4,128)S(1)}, u32[]{:S(2)}, u32[]{:S(2)}) async-start(f32[128,4,128]{2,1,0:T(4,128)} %bitcast.58), calls=%async_computation.2 | async-start | bytes 524288 | tf_op jit(solution)/shard_map/all_to_all | solution.py:254
  96.1 4.5 %extinction.1 = f32[4,2048,128]{2,1,0:T(8,128)} custom-call(f32[256,128]{1,0:T(8,128)} %bitcast.55, f32[8512,128]{1,0:T(8,128)} %get-tuple-element.25.refs_3_.refs_1_), custom_call_target="tpu_custom_call" | custom-call | flops 800000000 | bytes 8388608 | tf_op jit(solution)/shard_map/extinction/pallas_call | solution.py:465
  100.6 0.7 all-to-all-done.2
  101.3 0.7 scan.3
  102.0 10.3 %all-to-all-start.3 = ((f32[128,2,128]{2,1,0:T(2,128)}), f32[128,2,128]{2,1,0:T(2,128)S(1)}, u32[]{:S(2)}, u32[]{:S(2)}) async-start(f32[128,2,128]{2,1,0:T(2,128)} %bitcast.26), calls=%async_computation.3 | async-start | bytes 262144 | tf_op jit(solution)/shard_map/all_to_all | solution.py:254
  112.4 22.8 %spread.1.refs_2_ = f32[8512,128]{1,0:T(8,128)} custom-call(s32[128]{0:T(128)} %get-tuple-element.22.refs_0_.order_ref, s32[128]{0:T(128)} %get-tuple-element.23.refs_1_.count_ref, s32[128,128]{1,0:T(8,128)} %get-tuple-element.24.refs_2_.refs_0_, s32[128,128]{1,0:T(8,128)} %get-tuple-element.26.refs_4_.refs_1_, f32[128,128]{1,0:T(8,128)} %get-tuple-element.32.refs_2_, ...), custom_call_target="tpu_custom_call" | custom-call | flops 6000000000 | bytes 5242880 | tf_op jit(solution)/shard_map/spread/pallas_call | solution.py:406
  135.1 0.0 all-to-all-done.3
  135.2 0.6 copy-done.2
  135.8 6.4 %sensitivity.1 = f32[4,2048,128]{2,1,0:T(8,128)} custom-call(f32[256,128]{1,0:T(8,128)} %bitcast.56, f32[8192,128]{1,0:T(8,128)} %get-tuple-element.31.refs_1_, f32[8512,128]{1,0:T(8,128)} %spread.1.refs_2_), custom_call_target="tpu_custom_call" | custom-call | flops 1000000000 | bytes 12582912 | tf_op jit(solution)/shard_map/sensitivity/pallas_call | solution.py:515
  (3 shorter events, 0.0 us)
Async XLA Ops:
  2.4 14.7 %collective-permute-start.1 = (f32[256,4,128]{2,1,0:T(4,128)S(1)}, f32[256,4,128]{2,1,0:T(4,128)S(1)}, u32[]{:S(2)}, u32[]{:S(2)}) collective-permute-start(f32[256,4,128]{2,1,0:T(4,128)S(1)} %get-tuple-element.43), channel_id=1, source_target_pairs={{2,0},{4,2},{6,4},{8,6},{10,8},{12,10},{14,12},{16,14},{18,16},{20... | collective-permute-start | bytes 1572872 | tf_op jit(solution)/shard_map/ppermute | solution.py:574
  4.3 14.6 %collective-permute-start = (f32[256,4,128]{2,1,0:T(4,128)S(1)}, f32[256,4,128]{2,1,0:T(4,128)S(1)}, u32[]{:S(2)}, u32[]{:S(2)}) collective-permute-start(f32[256,4,128]{2,1,0:T(4,128)S(1)} %get-tuple-element.44), channel_id=1, source_target_pairs={{0,2},{2,4},{4,6},{6,8},{8,10},{10,12},{12,14},{14,16},{16,18},{18... | collective-permute-start | bytes 1572872 | tf_op jit(solution)/shard_map/ppermute | solution.py:573
  17.1 1.8 %copy-start.3 = (f32[256,4,128]{2,1,0:T(4,128)}, f32[256,4,128]{2,1,0:T(4,128)S(1)}, u32[]{:S(2)}) copy-start(f32[256,4,128]{2,1,0:T(4,128)S(1)} %collective-permute-done.1) | copy-start | bytes 1572868
  18.9 0.8 copy-start.4
  26.5 26.0 %all-to-all-start = ((f32[128,4,128]{2,1,0:T(4,128)}), f32[128,4,128]{2,1,0:T(4,128)S(1)}, u32[]{:S(2)}, u32[]{:S(2)}) async-start(f32[128,4,128]{2,1,0:T(4,128)} %bitcast.59), calls=%async_computation | async-start | bytes 524288 | tf_op jit(solution)/shard_map/all_to_all | solution.py:254
  52.6 21.8 %copy-start = (f32[128,4,128]{2,1,0:T(4,128)}, f32[128,4,128]{2,1,0:T(4,128)S(1)}, u32[]{:S(2)}) copy-start(f32[128,4,128]{2,1,0:T(4,128)S(1)} %all-to-all-done) | copy-start | bytes 786436
  53.3 21.1 %all-to-all-start.1 = ((f32[128,2,128]{2,1,0:T(2,128)}), f32[128,2,128]{2,1,0:T(2,128)S(1)}, u32[]{:S(2)}, u32[]{:S(2)}) async-start(f32[128,2,128]{2,1,0:T(2,128)} %bitcast.18), calls=%async_computation.1 | async-start | bytes 262144 | tf_op jit(solution)/shard_map/all_to_all | solution.py:254
  74.4 0.6 copy-start.1
  85.5 15.8 %all-to-all-start.2 = ((f32[128,4,128]{2,1,0:T(4,128)}), f32[128,4,128]{2,1,0:T(4,128)S(1)}, u32[]{:S(2)}, u32[]{:S(2)}) async-start(f32[128,4,128]{2,1,0:T(4,128)} %bitcast.58), calls=%async_computation.2 | async-start | bytes 524288 | tf_op jit(solution)/shard_map/all_to_all | solution.py:254
  102.0 33.1 %all-to-all-start.3 = ((f32[128,2,128]{2,1,0:T(2,128)}), f32[128,2,128]{2,1,0:T(2,128)S(1)}, u32[]{:S(2)}, u32[]{:S(2)}) async-start(f32[128,2,128]{2,1,0:T(2,128)} %bitcast.26), calls=%async_computation.3 | async-start | bytes 262144 | tf_op jit(solution)/shard_map/all_to_all | solution.py:254
  135.2 0.7 copy-start.2

commit v5 on v4

--- a/solution.py
+++ b/solution.py
@@ -13,7 +13,7 @@
 ACCS = 6
 TEAM = 4
 PAIR = 2
-STEP = 32
+STEP = 16
 CHUNKS = 8
 SPLIT = 7
 PACK = 64
@@ -54,7 +54,7 @@
 
 
 def density_kernel(shells, groups, devices, thickness, edge_ref, obs_ref, inv_ref, exc_hbm, up_hbm, down_hbm,
-                   dens_hbm, tab_hbm, pay_ref, exc_ref, up_ref, down_ref, dens_ref, tab_ref, in_sem, out_sem):
+                   tab_hbm, pay_ref, exc_ref, up_ref, down_ref, tab_ref, in_sem, out_sem):
     tall = shells + 1
     per = groups // CHUNKS
     weight = [v * LOG2E for v in taps()]
@@ -71,12 +71,8 @@
         ]
 
     def outputs(i):
-        flat = pl.ds(i * per * shells, per * shells)
         tall_rows = pl.ds(LEAD + i * per * tall, per * tall)
-        return [
-            pltpu.make_async_copy(dens_ref.at[flat, :], dens_hbm.at[flat, :], out_sem.at[0, i]),
-            pltpu.make_async_copy(tab_ref.at[tall_rows, :], tab_hbm.at[tall_rows, :], out_sem.at[1, i]),
-        ]
+        return [pltpu.make_async_copy(tab_ref.at[tall_rows, :], tab_hbm.at[tall_rows, :], out_sem.at[i])]
 
     for i in range(CHUNKS):
         for copy in inputs(i):
@@ -102,9 +98,7 @@
             value = weight[0] * exc[r]
             for k in range(1, PASSES + 1):
                 value = value + weight[k] * (exc[r - k] + exc[r + k])
-            dens = jnp.exp2(value)
-            dens_ref[pl.ds((g * shells + r) * SUB, SUB), :] = dens
-            step = dens * thickness
+            step = jnp.exp2(value) * thickness
             total = step if total is None else total + step
             tab_ref[pl.ds(LEAD + g * SUB * tall + 1 + r, SUB, stride=tall), :] = total
         first = g * SUB
@@ -131,9 +125,8 @@
     return pl.pallas_call(
         lambda *refs: density_kernel(shells, groups, devices, thickness, *refs),
         in_specs=[SMEM, VMEM, VMEM, ANY, ANY, ANY],
-        out_specs=[ANY, ANY, VMEM],
+        out_specs=[ANY, VMEM],
         out_shape=[
-            jax.ShapeDtypeStruct((groups * shells, LANES), jnp.float32),
             jax.ShapeDtypeStruct((rows, LANES), jnp.float32),
             jax.ShapeDtypeStruct((devices * FIELDS, LANES), jnp.float32),
         ],
@@ -141,10 +134,9 @@
             pltpu.VMEM(exc.shape, jnp.float32),
             pltpu.VMEM(up.shape, jnp.float32),
             pltpu.VMEM(down.shape, jnp.float32),
-            pltpu.VMEM((groups * shells, LANES), jnp.float32),
             pltpu.VMEM((rows, LANES), jnp.float32),
             pltpu.SemaphoreType.DMA((3, CHUNKS)),
-            pltpu.SemaphoreType.DMA((2, CHUNKS)),
+            pltpu.SemaphoreType.DMA((CHUNKS,)),
         ],
         cost_estimate=cost(8, 12 << 20),
         name="density",
@@ -166,15 +158,9 @@
     return copies
 
 
-def lookup_kernel(part, parts, chained, order_ref, count_ref, *refs):
-    n = 5 if chained else 4
-    out_ref = refs[n]
-    sources, targets, sem = refs[:n], refs[n + 1:-1], refs[-1]
-    idx_ref, tab_ref, low_ref, frac_ref = targets
-    if not chained:
-        out_ref[...] = jnp.zeros_like(out_ref)
-    for copy in fetch(sources, targets + ((out_ref,) if chained else ()), sem):
-        copy.wait()
+def lookup_kernel(part, parts, chained, order_ref, count_ref, idx_ref, tab_ref, low_ref, frac_ref, *refs):
+    out_ref = refs[-1]
+    out_ref[...] = refs[0][...] if chained else jnp.zeros_like(out_ref)
     lane = lax.broadcasted_iota(jnp.int32, (SUB, LANES), 1)
     sub = lax.broadcasted_iota(jnp.int32, (SUB, LANES), 0)
     pair = [(sub >> 1) == j for j in range(4)]
@@ -211,15 +197,8 @@
     return pl.pallas_call(
         lambda *refs: lookup_kernel(part, parts, column is not None, *refs),
         out_shape=jax.ShapeDtypeStruct(low.shape, jnp.float32),
-        in_specs=[SMEM, SMEM] + [ANY] * (4 + len(extra)),
+        in_specs=[SMEM, SMEM, SMEM] + [VMEM] * (3 + len(extra)),
         out_specs=VMEM,
-        scratch_shapes=[
-            pltpu.SMEM(idx.shape, jnp.int32),
-            pltpu.VMEM(tab.shape, jnp.float32),
-            pltpu.VMEM(low.shape, jnp.int32),
-            pltpu.VMEM(frac.shape, jnp.float32),
-            pltpu.SemaphoreType.DMA((4 + len(extra),)),
-        ],
         cost_estimate=cost(12, 5 << 20),
         name="lookup",
     )(order, counts, idx, tab, low, frac, *extra)
@@ -478,7 +457,7 @@
     )(off, tab)
 
 
-def sensitivity_kernel(shells, devices, off_ref, dens_hbm, drop_hbm, out_hbm, dens_ref, drop_ref, out_ref,
+def sensitivity_kernel(shells, devices, thickness, off_ref, tab_hbm, drop_hbm, out_hbm, tab_ref, drop_ref, out_ref,
                        in_sem, out_sem):
     tall = shells + 1
     groups = off_ref.shape[0]
@@ -486,10 +465,9 @@
     per = groups // CHUNKS
 
     def inputs(i):
-        flat = pl.ds(i * per * shells, per * shells)
         rows = pl.ds(LEAD + i * per * tall, per * tall)
         return [
-            pltpu.make_async_copy(dens_hbm.at[flat, :], dens_ref.at[flat, :], in_sem.at[0, i]),
+            pltpu.make_async_copy(tab_hbm.at[rows, :], tab_ref.at[rows, :], in_sem.at[0, i]),
             pltpu.make_async_copy(drop_hbm.at[rows, :], drop_ref.at[rows, :], in_sem.at[1, i]),
         ]
 
@@ -502,23 +480,27 @@
             g = i * (per // SUB) + k
             first = g * SUB
             total = off_ref[pl.ds((first % devices) * share + first // devices, SUB, stride=share), :]
+            scale = 1.0 / thickness
+            outer = tab_ref[pl.ds(LEAD + g * SUB * tall + shells, SUB, stride=tall), :]
             for r in range(shells - 1, -1, -1):
+                inner = tab_ref[pl.ds(LEAD + g * SUB * tall + r, SUB, stride=tall), :]
                 total = total + drop_ref[pl.ds(LEAD + g * SUB * tall + 1 + r, SUB, stride=tall), :]
                 out_ref.at[r // SUB][pl.ds(g * SUB * SUB + r % SUB, SUB, stride=SUB), :] = (
-                    dens_ref[pl.ds((g * shells + r) * SUB, SUB), :] * total)
+                    (outer - inner) * scale * total)
+                outer = inner
 
     chunked(work, inputs, outputs)
 
 
-def sensitivity_call(dens, drop, off, shells, devices):
+def sensitivity_call(tab, drop, off, shells, devices, thickness):
     shape = (shells // SUB, off.shape[0] * SUB, LANES)
     return pl.pallas_call(
-        lambda *refs: sensitivity_kernel(shells, devices, *refs),
+        lambda *refs: sensitivity_kernel(shells, devices, thickness, *refs),
         in_specs=[VMEM, ANY, ANY],
         out_specs=ANY,
         out_shape=jax.ShapeDtypeStruct(shape, jnp.float32),
         scratch_shapes=[
-            pltpu.VMEM(dens.shape, jnp.float32),
+            pltpu.VMEM(tab.shape, jnp.float32),
             pltpu.VMEM(drop.shape, jnp.float32),
             pltpu.VMEM(shape, jnp.float32),
             pltpu.SemaphoreType.DMA((2, CHUNKS)),
@@ -526,7 +508,7 @@
         ],
         cost_estimate=cost(5, 12 << 20),
         name="sensitivity",
-    )(off, dens, drop)
+    )(off, tab, drop)
 
 
 def to_tiles(x):
@@ -580,7 +562,7 @@
     from_below, from_above, idx, low, order, counts = lax.optimization_barrier(
         (from_below, from_above, idx, low, order, counts))
     edge = jnp.stack(((me == 0).astype(jnp.float32), (me == blocks - 1).astype(jnp.float32)))
-    dens, tab, parts = density_call(
+    tab, parts = density_call(
         to_tiles(excitation),
         from_below.reshape(groups * PASSES, LANES),
         from_above.reshape(groups * PASSES, LANES),
@@ -599,7 +581,7 @@
 
     rows = table_rows(groups, tall)
     drop = spread_call(order, counts, idx, low, here, inner, rows)
-    sensitivity = sensitivity_call(dens, drop, tail_offset, shells, devices)
+    sensitivity = sensitivity_call(tab, drop, tail_offset, shells, devices, thickness)
     return from_tiles(extinction), from_tiles(sensitivity), residual[:, None, :]
 
 

time: 144 us -> 144 us (level)
  starting transfers between devices: 52.3 us -> 49.7 us
  Pallas kernels: 73.4 us -> 75.7 us
    all_to_all x4, starting transfers between devices: 47 us -> 44.4 us  [exchange(): parts = lax.all_to_all(parts, BOTH, split_axis=0, concat_axis=0, tiled=True)]
    pallas_call x1, Pallas kernels: 22.8 us -> 25 us  [spread_call(): pl.pallas_call(spread_kernel, out_shape=jax.ShapeDtypeStruct(shape, jnp.f...]
  transfers between devices with their start and end apart: 6 -> 6, of which waited for: 3 -> 3; matrix products, arithmetic and copies ran while one was open for 3% -> 3% of each run, Pallas kernels for 34% -> 36%
where the time goes in v5:
time: 144 us; the launch traced here: 142 us
  Pallas kernels  75.7 us (53%)
  starting transfers between devices  49.7 us (35%)
  waiting for transfers between devices  8.21 us (6%)
  local copies, waits for them, and re-layouts  3.81 us (3%)
  other arithmetic  3.69 us (3%)
    all_to_all x4, starting transfers between devices, exchange(): parts = lax.all_to_all(parts, BOTH, split_axis=0, concat_axis=0, tiled=True)  44.4 us
    pallas_call x1, Pallas kernels, spread_call(): pl.pallas_call(spread_kernel, out_shape=jax.ShapeDtypeStruct(shape, jnp.f...  25 us
    pallas_call x2, Pallas kernels, lookup_call(): pl.pallas_call(lambda *refs: lookup_kernel(part, parts, column is not Non...  21.5 us
    pallas_call x1, Pallas kernels, star_call(): pl.pallas_call(lambda *refs: star_kernel(devices, *refs), out_shape=[jax....  10.4 us
    pallas_call x1, Pallas kernels, sensitivity_call(): pl.pallas_call(lambda *refs: sensitivity_kernel(shells, devices, thicknes...  6.43 us
    pallas_call x1, Pallas kernels, density_call(): pl.pallas_call(lambda *refs: density_kernel(shells, groups, devices, thic...  6.39 us
    ppermute x1, waiting for transfers between devices, body(): lax.ppermute(edge_rows(excitation, slice(0, PASSES)), 'shell', down)  5.69 us
    pallas_call x1, Pallas kernels, extinction_call(): pl.pallas_call(lambda *refs: extinction_kernel(shells, devices, *refs), i...  4.48 us
  transfers between devices with their start and end apart: 6, of which 3 were waited for; matrix products, arithmetic and copies ran while one was open for 3% of the time, Pallas kernels for 36%

profile of v5, /device:TPU:87, one launch (start us, length us, event | category | flops | bytes accessed | tf_op | source)
XLA Modules:
  0.0 141.8 jit_solution(4685200097247477152)
XLA Ops:
  0.6 1.7 %slice_bitcast_fusion = (f32[256,4,128]{2,1,0:T(4,128)S(1)}, f32[256,4,128]{2,1,0:T(4,128)S(1)}) fusion(f32[32,32768]{1,0:T(8,128)} %param.7), kind=kLoop, calls=%fused_computation | loop fusion | bytes 2097152 | tf_op jit(solution)/shard_map/transpose | solution.py:530
  2.4 1.9 %collective-permute-start.1 = (f32[256,4,128]{2,1,0:T(4,128)S(1)}, f32[256,4,128]{2,1,0:T(4,128)S(1)}, u32[]{:S(2)}, u32[]{:S(2)}) collective-permute-start(f32[256,4,128]{2,1,0:T(4,128)S(1)} %get-tuple-element.41), channel_id=1, source_target_pairs={{2,0},{4,2},{6,4},{8,6},{10,8},{12,10},{14,12},{16,14},{18,16},{20... | collective-permute-start | bytes 1572872 | tf_op jit(solution)/shard_map/ppermute | solution.py:556
  4.3 3.4 %collective-permute-start = (f32[256,4,128]{2,1,0:T(4,128)S(1)}, f32[256,4,128]{2,1,0:T(4,128)S(1)}, u32[]{:S(2)}, u32[]{:S(2)}) collective-permute-start(f32[256,4,128]{2,1,0:T(4,128)S(1)} %get-tuple-element.42), channel_id=1, source_target_pairs={{0,2},{2,4},{4,6},{6,8},{8,10},{10,12},{12,14},{14,16},{16,18},{18... | collective-permute-start | bytes 1572872 | tf_op jit(solution)/shard_map/ppermute | solution.py:555
  7.7 0.7 add_convert_fusion.refs_0_
  8.3 0.9 convert_reduce_fusion
  9.2 2.1 %select_reduce_fusion = (s32[128]{0:T(128)}, s32[128]{0:T(128)}, s32[128,128]{1,0:T(8,128)}, s32[128,128]{1,0:T(8,128)}) fusion(s32[128]{0:T(128)S(1)} %convert_reduce_fusion, s32[128]{0:T(128)} %bitcast.62, s32[1,128,128]{2,1,0:T(8,128)} %param.8, s32[1,128,128]{2,1,0:T(8,128)} %param.9), kind=kLoop, calls=%fused_computation.4 | loop fusion | flops 163584 | bytes 264192 | tf_op jit(solution)/shard_map/reduce_sum | solution.py:541
  11.4 5.7 %collective-permute-done.1 = f32[256,4,128]{2,1,0:T(4,128)S(1)} collective-permute-done((f32[256,4,128]{2,1,0:T(4,128)S(1)}, f32[256,4,128]{2,1,0:T(4,128)S(1)}, u32[]{:S(2)}, u32[]{:S(2)}) %collective-permute-start.1) | collective-permute-done | bytes 524320 | tf_op jit(solution)/shard_map/ppermute | solution.py:556
  17.1 1.8 %collective-permute-done = f32[256,4,128]{2,1,0:T(4,128)S(1)} collective-permute-done((f32[256,4,128]{2,1,0:T(4,128)S(1)}, f32[256,4,128]{2,1,0:T(4,128)S(1)}, u32[]{:S(2)}, u32[]{:S(2)}) %collective-permute-start) | collective-permute-done | bytes 524320 | tf_op jit(solution)/shard_map/ppermute | solution.py:555
  18.9 0.0 copy-done.3
  18.9 0.8 copy-done.4
  19.7 6.4 %density.1 = (f32[8512,128]{1,0:T(8,128)}, f32[512,128]{1,0:T(8,128)}) custom-call(f32[2]{0:T(128)} %add_convert_fusion.refs_0_, f32[128,128]{1,0:T(8,128)} %bitcast.65, f32[128,128]{1,0:T(8,128)} %bitcast.66, f32[4,2048,128]{2,1,0:T(8,128)} %bitcast.57, f32[1024,128]{1,0:T(8,128)} %bitcast.64, f32[1024,128]{1,0:T(8,128)} %bitcast.63), custom_call_target="tpu_custom_call" | custom-call | flops 1600000000 | bytes 12582912 | tf_op jit(solution)/shard_map/density/pallas_call | solution.py:125
  26.1 15.4 %all-to-all-start = ((f32[128,4,128]{2,1,0:T(4,128)}), f32[128,4,128]{2,1,0:T(4,128)S(1)}, u32[]{:S(2)}, u32[]{:S(2)}) async-start(f32[128,4,128]{2,1,0:T(4,128)} %bitcast.59), calls=%async_computation | async-start | bytes 524288 | tf_op jit(solution)/shard_map/all_to_all | solution.py:233
  41.5 10.8 %lookup.2.refs_6_ = f32[128,128]{1,0:T(8,128)} custom-call(s32[128]{0:T(128)} %get-tuple-element.21.refs_0_.order_ref, s32[128]{0:T(128)} %get-tuple-element.22.refs_1_.count_ref, s32[128,128]{1,0:T(8,128)} %get-tuple-element.23.refs_2_.refs_0_, f32[8512,128]{1,0:T(8,128)} %get-tuple-element.24.refs_3_.refs_1_, ...), custom_call_target="tpu_custom_call" | custom-call | flops 2400000000 | bytes 5242880 | tf_op jit(solution)/shard_map/lookup/pallas_call | solution.py:197
  52.2 0.0 all-to-all-done
  52.2 0.7 scan.2
  53.0 9.3 %all-to-all-start.1 = ((f32[128,2,128]{2,1,0:T(2,128)}), f32[128,2,128]{2,1,0:T(2,128)S(1)}, u32[]{:S(2)}, u32[]{:S(2)}) async-start(f32[128,2,128]{2,1,0:T(2,128)} %bitcast.18), calls=%async_computation.1 | async-start | bytes 262144 | tf_op jit(solution)/shard_map/all_to_all | solution.py:233
  62.3 10.7 %lookup.3.refs_4_ = f32[128,128]{1,0:T(8,128)} custom-call(s32[128]{0:T(128)} %get-tuple-element.21.refs_0_.order_ref, s32[128]{0:T(128)} %get-tuple-element.22.refs_1_.count_ref, s32[128,128]{1,0:T(8,128)} %get-tuple-element.23.refs_2_.refs_0_, f32[8512,128]{1,0:T(8,128)} %get-tuple-element.24.refs_3_.refs_1_, ...), custom_call_target="tpu_custom_call" | custom-call | flops 2400000000 | bytes 5242880 | tf_op jit(solution)/shard_map/lookup/pallas_call | solution.py:197
  73.1 0.0 copy-done
  73.1 0.0 all-to-all-done.1
  73.1 0.0 copy-start.1
  73.1 0.6 copy-done.1
  73.7 10.4 %star.1 = (f32[512,128]{1,0:T(8,128)}, f32[128,128]{1,0:T(8,128)}, f32[128,128]{1,0:T(8,128)}) custom-call(s32[1,128]{1,0:T(1,128)} %refs_0_.1, s32[128,128]{1,0:T(8,128)} %bitcast.60, f32[256,128]{1,0:T(8,128)} %bitcast.54, f32[512,128]{1,0:T(8,128)} %bitcast.50, f32[128,128]{1,0:T(8,128)} %lookup.3.refs_4_, f32[128,128]{1,0:T(8,128)} %bitcast.69), custom_call_target="tpu_custom_call" | custom-call | flops 1600000000 | bytes 1048576 | tf_op jit(solution)/shard_map/star/pallas_call | solution.py:303
  84.1 9.3 %all-to-all-start.2 = ((f32[128,4,128]{2,1,0:T(4,128)}), f32[128,4,128]{2,1,0:T(4,128)S(1)}, u32[]{:S(2)}, u32[]{:S(2)}) async-start(f32[128,4,128]{2,1,0:T(4,128)} %bitcast.58), calls=%async_computation.2 | async-start | bytes 524288 | tf_op jit(solution)/shard_map/all_to_all | solution.py:233
  93.4 4.5 %extinction.1 = f32[4,2048,128]{2,1,0:T(8,128)} custom-call(f32[256,128]{1,0:T(8,128)} %bitcast.55, f32[8512,128]{1,0:T(8,128)} %get-tuple-element.24.refs_3_.refs_1_), custom_call_target="tpu_custom_call" | custom-call | flops 800000000 | bytes 8388608 | tf_op jit(solution)/shard_map/extinction/pallas_call | solution.py:444
  97.9 0.7 all-to-all-done.2
  98.6 0.7 scan.3
  99.3 10.3 %all-to-all-start.3 = ((f32[128,2,128]{2,1,0:T(2,128)}), f32[128,2,128]{2,1,0:T(2,128)S(1)}, u32[]{:S(2)}, u32[]{:S(2)}) async-start(f32[128,2,128]{2,1,0:T(2,128)} %bitcast.26), calls=%async_computation.3 | async-start | bytes 262144 | tf_op jit(solution)/shard_map/all_to_all | solution.py:233
  109.7 25.0 %spread.1.refs_2_ = f32[8512,128]{1,0:T(8,128)} custom-call(s32[128]{0:T(128)} %get-tuple-element.21.refs_0_.order_ref, s32[128]{0:T(128)} %get-tuple-element.22.refs_1_.count_ref, s32[128,128]{1,0:T(8,128)} %get-tuple-element.23.refs_2_.refs_0_, s32[128,128]{1,0:T(8,128)} %get-tuple-element.25.refs_4_.refs_1_, f32[128,128]{1,0:T(8,128)} %get-tuple-element.30.refs_2_, ...), custom_call_target="tpu_custom_call" | custom-call | flops 6000000000 | bytes 5242880 | tf_op jit(solution)/shard_map/spread/pallas_call | solution.py:385
  134.7 0.0 all-to-all-done.3
  134.7 0.0 copy-start.2
  134.7 0.6 copy-done.2
  135.4 6.4 %sensitivity.1 = f32[4,2048,128]{2,1,0:T(8,128)} custom-call(f32[256,128]{1,0:T(8,128)} %bitcast.56, f32[8512,128]{1,0:T(8,128)} %get-tuple-element.24.refs_3_.refs_1_, f32[8512,128]{1,0:T(8,128)} %spread.1.refs_2_), custom_call_target="tpu_custom_call" | custom-call | flops 1000000000 | bytes 12582912 | tf_op jit(solution)/shard_map/sensitivity/pallas_call | solution.py:497
  (3 shorter events, 0.0 us)
Async XLA Ops:
  2.4 14.7 %collective-permute-start.1 = (f32[256,4,128]{2,1,0:T(4,128)S(1)}, f32[256,4,128]{2,1,0:T(4,128)S(1)}, u32[]{:S(2)}, u32[]{:S(2)}) collective-permute-start(f32[256,4,128]{2,1,0:T(4,128)S(1)} %get-tuple-element.41), channel_id=1, source_target_pairs={{2,0},{4,2},{6,4},{8,6},{10,8},{12,10},{14,12},{16,14},{18,16},{20... | collective-permute-start | bytes 1572872 | tf_op jit(solution)/shard_map/ppermute | solution.py:556
  4.3 14.6 %collective-permute-start = (f32[256,4,128]{2,1,0:T(4,128)S(1)}, f32[256,4,128]{2,1,0:T(4,128)S(1)}, u32[]{:S(2)}, u32[]{:S(2)}) collective-permute-start(f32[256,4,128]{2,1,0:T(4,128)S(1)} %get-tuple-element.42), channel_id=1, source_target_pairs={{0,2},{2,4},{4,6},{6,8},{8,10},{10,12},{12,14},{14,16},{16,18},{18... | collective-permute-start | bytes 1572872 | tf_op jit(solution)/shard_map/ppermute | solution.py:555
  17.1 1.8 %copy-start.3 = (f32[256,4,128]{2,1,0:T(4,128)}, f32[256,4,128]{2,1,0:T(4,128)S(1)}, u32[]{:S(2)}) copy-start(f32[256,4,128]{2,1,0:T(4,128)S(1)} %collective-permute-done.1) | copy-start | bytes 1572868
  18.9 0.8 copy-start.4
  26.1 26.2 %all-to-all-start = ((f32[128,4,128]{2,1,0:T(4,128)}), f32[128,4,128]{2,1,0:T(4,128)S(1)}, u32[]{:S(2)}, u32[]{:S(2)}) async-start(f32[128,4,128]{2,1,0:T(4,128)} %bitcast.59), calls=%async_computation | async-start | bytes 524288 | tf_op jit(solution)/shard_map/all_to_all | solution.py:233
  52.2 20.8 %copy-start = (f32[128,4,128]{2,1,0:T(4,128)}, f32[128,4,128]{2,1,0:T(4,128)S(1)}, u32[]{:S(2)}) copy-start(f32[128,4,128]{2,1,0:T(4,128)S(1)} %all-to-all-done) | copy-start | bytes 786436
  53.0 20.1 %all-to-all-start.1 = ((f32[128,2,128]{2,1,0:T(2,128)}), f32[128,2,128]{2,1,0:T(2,128)S(1)}, u32[]{:S(2)}, u32[]{:S(2)}) async-start(f32[128,2,128]{2,1,0:T(2,128)} %bitcast.18), calls=%async_computation.1 | async-start | bytes 262144 | tf_op jit(solution)/shard_map/all_to_all | solution.py:233
  73.1 0.6 copy-start.1
  84.1 14.5 %all-to-all-start.2 = ((f32[128,4,128]{2,1,0:T(4,128)}), f32[128,4,128]{2,1,0:T(4,128)S(1)}, u32[]{:S(2)}, u32[]{:S(2)}) async-start(f32[128,4,128]{2,1,0:T(4,128)} %bitcast.58), calls=%async_computation.2 | async-start | bytes 524288 | tf_op jit(solution)/shard_map/all_to_all | solution.py:233
  99.3 35.4 %all-to-all-start.3 = ((f32[128,2,128]{2,1,0:T(2,128)}), f32[128,2,128]{2,1,0:T(2,128)S(1)}, u32[]{:S(2)}, u32[]{:S(2)}) async-start(f32[128,2,128]{2,1,0:T(2,128)} %bitcast.26), calls=%async_computation.3 | async-start | bytes 262144 | tf_op jit(solution)/shard_map/all_to_all | solution.py:233
  134.7 0.7 copy-start.2

commit v6 on v5

--- a/solution.py
+++ b/solution.py
@@ -13,7 +13,7 @@
 ACCS = 6
 TEAM = 4
 PAIR = 2
-STEP = 16
+STEP = 32
 CHUNKS = 8
 SPLIT = 7
 PACK = 64

time: 144 us -> 143 us (level)
  transfers between devices with their start and end apart: 6 -> 6, of which waited for: 3 -> 3; matrix products, arithmetic and copies ran while one was open for 3% -> 3% of each run, Pallas kernels for 36% -> 35%
where the time goes in v6:
time: 143 us; the launch traced here: 141 us
  Pallas kernels  74.6 us (52%)
  starting transfers between devices  50.1 us (35%)
  waiting for transfers between devices  8.21 us (6%)
  local copies, waits for them, and re-layouts  3.81 us (3%)
  other arithmetic  3.69 us (3%)
    all_to_all x4, starting transfers between devices, exchange(): parts = lax.all_to_all(parts, BOTH, split_axis=0, concat_axis=0, tiled=True)  44.8 us
    pallas_call x1, Pallas kernels, spread_call(): pl.pallas_call(spread_kernel, out_shape=jax.ShapeDtypeStruct(shape, jnp.f...  24.3 us
    pallas_call x2, Pallas kernels, lookup_call(): pl.pallas_call(lambda *refs: lookup_kernel(part, parts, column is not Non...  21.1 us
    pallas_call x1, Pallas kernels, star_call(): pl.pallas_call(lambda *refs: star_kernel(devices, *refs), out_shape=[jax....  10.4 us
    pallas_call x1, Pallas kernels, sensitivity_call(): pl.pallas_call(lambda *refs: sensitivity_kernel(shells, devices, thicknes...  6.43 us
    pallas_call x1, Pallas kernels, density_call(): pl.pallas_call(lambda *refs: density_kernel(shells, groups, devices, thic...  6.39 us
    ppermute x1, waiting for transfers between devices, body(): lax.ppermute(edge_rows(excitation, slice(0, PASSES)), 'shell', down)  5.69 us
    pallas_call x1, Pallas kernels, extinction_call(): pl.pallas_call(lambda *refs: extinction_kernel(shells, devices, *refs), i...  4.48 us
  transfers between devices with their start and end apart: 6, of which 3 were waited for; matrix products, arithmetic and copies ran while one was open for 3% of the time, Pallas kernels for 35%

profile of v6, /device:TPU:87, one launch (start us, length us, event | category | flops | bytes accessed | tf_op | source)
XLA Modules:
  0.0 141.1 jit_solution(6343664288931288273)
XLA Ops:
  0.6 1.7 %slice_bitcast_fusion = (f32[256,4,128]{2,1,0:T(4,128)S(1)}, f32[256,4,128]{2,1,0:T(4,128)S(1)}) fusion(f32[32,32768]{1,0:T(8,128)} %param.7), kind=kLoop, calls=%fused_computation | loop fusion | bytes 2097152 | tf_op jit(solution)/shard_map/transpose | solution.py:530
  2.4 1.9 %collective-permute-start.1 = (f32[256,4,128]{2,1,0:T(4,128)S(1)}, f32[256,4,128]{2,1,0:T(4,128)S(1)}, u32[]{:S(2)}, u32[]{:S(2)}) collective-permute-start(f32[256,4,128]{2,1,0:T(4,128)S(1)} %get-tuple-element.41), channel_id=1, source_target_pairs={{2,0},{4,2},{6,4},{8,6},{10,8},{12,10},{14,12},{16,14},{18,16},{20... | collective-permute-start | bytes 1572872 | tf_op jit(solution)/shard_map/ppermute | solution.py:556
  4.3 3.4 %collective-permute-start = (f32[256,4,128]{2,1,0:T(4,128)S(1)}, f32[256,4,128]{2,1,0:T(4,128)S(1)}, u32[]{:S(2)}, u32[]{:S(2)}) collective-permute-start(f32[256,4,128]{2,1,0:T(4,128)S(1)} %get-tuple-element.42), channel_id=1, source_target_pairs={{0,2},{2,4},{4,6},{6,8},{8,10},{10,12},{12,14},{14,16},{16,18},{18... | collective-permute-start | bytes 1572872 | tf_op jit(solution)/shard_map/ppermute | solution.py:555
  7.7 0.7 add_convert_fusion.refs_0_
  8.3 0.9 convert_reduce_fusion
  9.2 2.1 %select_reduce_fusion = (s32[128]{0:T(128)}, s32[128]{0:T(128)}, s32[128,128]{1,0:T(8,128)}, s32[128,128]{1,0:T(8,128)}) fusion(s32[128]{0:T(128)S(1)} %convert_reduce_fusion, s32[128]{0:T(128)} %bitcast.62, s32[1,128,128]{2,1,0:T(8,128)} %param.8, s32[1,128,128]{2,1,0:T(8,128)} %param.9), kind=kLoop, calls=%fused_computation.4 | loop fusion | flops 163584 | bytes 264192 | tf_op jit(solution)/shard_map/reduce_sum | solution.py:541
  11.4 5.7 %collective-permute-done.1 = f32[256,4,128]{2,1,0:T(4,128)S(1)} collective-permute-done((f32[256,4,128]{2,1,0:T(4,128)S(1)}, f32[256,4,128]{2,1,0:T(4,128)S(1)}, u32[]{:S(2)}, u32[]{:S(2)}) %collective-permute-start.1) | collective-permute-done | bytes 524320 | tf_op jit(solution)/shard_map/ppermute | solution.py:556
  17.1 1.8 %collective-permute-done = f32[256,4,128]{2,1,0:T(4,128)S(1)} collective-permute-done((f32[256,4,128]{2,1,0:T(4,128)S(1)}, f32[256,4,128]{2,1,0:T(4,128)S(1)}, u32[]{:S(2)}, u32[]{:S(2)}) %collective-permute-start) | collective-permute-done | bytes 524320 | tf_op jit(solution)/shard_map/ppermute | solution.py:555
  18.9 0.0 copy-done.3
  18.9 0.8 copy-done.4
  19.7 6.4 %density.1 = (f32[8512,128]{1,0:T(8,128)}, f32[512,128]{1,0:T(8,128)}) custom-call(f32[2]{0:T(128)} %add_convert_fusion.refs_0_, f32[128,128]{1,0:T(8,128)} %bitcast.65, f32[128,128]{1,0:T(8,128)} %bitcast.66, f32[4,2048,128]{2,1,0:T(8,128)} %bitcast.57, f32[1024,128]{1,0:T(8,128)} %bitcast.64, f32[1024,128]{1,0:T(8,128)} %bitcast.63), custom_call_target="tpu_custom_call" | custom-call | flops 1600000000 | bytes 12582912 | tf_op jit(solution)/shard_map/density/pallas_call | solution.py:125
  26.1 15.4 %all-to-all-start = ((f32[128,4,128]{2,1,0:T(4,128)}), f32[128,4,128]{2,1,0:T(4,128)S(1)}, u32[]{:S(2)}, u32[]{:S(2)}) async-start(f32[128,4,128]{2,1,0:T(4,128)} %bitcast.59), calls=%async_computation | async-start | bytes 524288 | tf_op jit(solution)/shard_map/all_to_all | solution.py:233
  41.5 10.7 %lookup.2.refs_6_ = f32[128,128]{1,0:T(8,128)} custom-call(s32[128]{0:T(128)} %get-tuple-element.21.refs_0_.order_ref, s32[128]{0:T(128)} %get-tuple-element.22.refs_1_.count_ref, s32[128,128]{1,0:T(8,128)} %get-tuple-element.23.refs_2_.refs_0_, f32[8512,128]{1,0:T(8,128)} %get-tuple-element.24.refs_3_.refs_1_, ...), custom_call_target="tpu_custom_call" | custom-call | flops 2400000000 | bytes 5242880 | tf_op jit(solution)/shard_map/lookup/pallas_call | solution.py:197
  52.1 0.0 all-to-all-done
  52.1 0.7 scan.2
  52.9 9.5 %all-to-all-start.1 = ((f32[128,2,128]{2,1,0:T(2,128)}), f32[128,2,128]{2,1,0:T(2,128)S(1)}, u32[]{:S(2)}, u32[]{:S(2)}) async-start(f32[128,2,128]{2,1,0:T(2,128)} %bitcast.18), calls=%async_computation.1 | async-start | bytes 262144 | tf_op jit(solution)/shard_map/all_to_all | solution.py:233
  62.4 10.4 %lookup.3.refs_4_ = f32[128,128]{1,0:T(8,128)} custom-call(s32[128]{0:T(128)} %get-tuple-element.21.refs_0_.order_ref, s32[128]{0:T(128)} %get-tuple-element.22.refs_1_.count_ref, s32[128,128]{1,0:T(8,128)} %get-tuple-element.23.refs_2_.refs_0_, f32[8512,128]{1,0:T(8,128)} %get-tuple-element.24.refs_3_.refs_1_, ...), custom_call_target="tpu_custom_call" | custom-call | flops 2400000000 | bytes 5242880 | tf_op jit(solution)/shard_map/lookup/pallas_call | solution.py:197
  72.9 0.0 copy-done
  72.9 0.0 all-to-all-done.1
  72.9 0.0 copy-start.1
  72.9 0.6 copy-done.1
  73.5 10.4 %star.1 = (f32[512,128]{1,0:T(8,128)}, f32[128,128]{1,0:T(8,128)}, f32[128,128]{1,0:T(8,128)}) custom-call(s32[1,128]{1,0:T(1,128)} %refs_0_.1, s32[128,128]{1,0:T(8,128)} %bitcast.60, f32[256,128]{1,0:T(8,128)} %bitcast.54, f32[512,128]{1,0:T(8,128)} %bitcast.50, f32[128,128]{1,0:T(8,128)} %lookup.3.refs_4_, f32[128,128]{1,0:T(8,128)} %bitcast.69), custom_call_target="tpu_custom_call" | custom-call | flops 1600000000 | bytes 1048576 | tf_op jit(solution)/shard_map/star/pallas_call | solution.py:303
  84.0 9.6 %all-to-all-start.2 = ((f32[128,4,128]{2,1,0:T(4,128)}), f32[128,4,128]{2,1,0:T(4,128)S(1)}, u32[]{:S(2)}, u32[]{:S(2)}) async-start(f32[128,4,128]{2,1,0:T(4,128)} %bitcast.58), calls=%async_computation.2 | async-start | bytes 524288 | tf_op jit(solution)/shard_map/all_to_all | solution.py:233
  93.5 4.5 %extinction.1 = f32[4,2048,128]{2,1,0:T(8,128)} custom-call(f32[256,128]{1,0:T(8,128)} %bitcast.55, f32[8512,128]{1,0:T(8,128)} %get-tuple-element.24.refs_3_.refs_1_), custom_call_target="tpu_custom_call" | custom-call | flops 800000000 | bytes 8388608 | tf_op jit(solution)/shard_map/extinction/pallas_call | solution.py:444
  98.0 0.7 all-to-all-done.2
  98.7 0.7 scan.3
  99.4 10.3 %all-to-all-start.3 = ((f32[128,2,128]{2,1,0:T(2,128)}), f32[128,2,128]{2,1,0:T(2,128)S(1)}, u32[]{:S(2)}, u32[]{:S(2)}) async-start(f32[128,2,128]{2,1,0:T(2,128)} %bitcast.26), calls=%async_computation.3 | async-start | bytes 262144 | tf_op jit(solution)/shard_map/all_to_all | solution.py:233
  109.8 24.3 %spread.1.refs_2_ = f32[8512,128]{1,0:T(8,128)} custom-call(s32[128]{0:T(128)} %get-tuple-element.21.refs_0_.order_ref, s32[128]{0:T(128)} %get-tuple-element.22.refs_1_.count_ref, s32[128,128]{1,0:T(8,128)} %get-tuple-element.23.refs_2_.refs_0_, s32[128,128]{1,0:T(8,128)} %get-tuple-element.25.refs_4_.refs_1_, f32[128,128]{1,0:T(8,128)} %get-tuple-element.30.refs_2_, ...), custom_call_target="tpu_custom_call" | custom-call | flops 6000000000 | bytes 5242880 | tf_op jit(solution)/shard_map/spread/pallas_call | solution.py:385
  134.0 0.0 all-to-all-done.3
  134.0 0.0 copy-start.2
  134.0 0.6 copy-done.2
  134.7 6.4 %sensitivity.1 = f32[4,2048,128]{2,1,0:T(8,128)} custom-call(f32[256,128]{1,0:T(8,128)} %bitcast.56, f32[8512,128]{1,0:T(8,128)} %get-tuple-element.24.refs_3_.refs_1_, f32[8512,128]{1,0:T(8,128)} %spread.1.refs_2_), custom_call_target="tpu_custom_call" | custom-call | flops 1000000000 | bytes 12582912 | tf_op jit(solution)/shard_map/sensitivity/pallas_call | solution.py:497
  (3 shorter events, 0.0 us)
Async XLA Ops:
  2.4 14.7 %collective-permute-start.1 = (f32[256,4,128]{2,1,0:T(4,128)S(1)}, f32[256,4,128]{2,1,0:T(4,128)S(1)}, u32[]{:S(2)}, u32[]{:S(2)}) collective-permute-start(f32[256,4,128]{2,1,0:T(4,128)S(1)} %get-tuple-element.41), channel_id=1, source_target_pairs={{2,0},{4,2},{6,4},{8,6},{10,8},{12,10},{14,12},{16,14},{18,16},{20... | collective-permute-start | bytes 1572872 | tf_op jit(solution)/shard_map/ppermute | solution.py:556
  4.3 14.6 %collective-permute-start = (f32[256,4,128]{2,1,0:T(4,128)S(1)}, f32[256,4,128]{2,1,0:T(4,128)S(1)}, u32[]{:S(2)}, u32[]{:S(2)}) collective-permute-start(f32[256,4,128]{2,1,0:T(4,128)S(1)} %get-tuple-element.42), channel_id=1, source_target_pairs={{0,2},{2,4},{4,6},{6,8},{8,10},{10,12},{12,14},{14,16},{16,18},{18... | collective-permute-start | bytes 1572872 | tf_op jit(solution)/shard_map/ppermute | solution.py:555
  17.1 1.8 %copy-start.3 = (f32[256,4,128]{2,1,0:T(4,128)}, f32[256,4,128]{2,1,0:T(4,128)S(1)}, u32[]{:S(2)}) copy-start(f32[256,4,128]{2,1,0:T(4,128)S(1)} %collective-permute-done.1) | copy-start | bytes 1572868
  18.9 0.8 copy-start.4
  26.1 26.1 %all-to-all-start = ((f32[128,4,128]{2,1,0:T(4,128)}), f32[128,4,128]{2,1,0:T(4,128)S(1)}, u32[]{:S(2)}, u32[]{:S(2)}) async-start(f32[128,4,128]{2,1,0:T(4,128)} %bitcast.59), calls=%async_computation | async-start | bytes 524288 | tf_op jit(solution)/shard_map/all_to_all | solution.py:233
  52.1 20.7 %copy-start = (f32[128,4,128]{2,1,0:T(4,128)}, f32[128,4,128]{2,1,0:T(4,128)S(1)}, u32[]{:S(2)}) copy-start(f32[128,4,128]{2,1,0:T(4,128)S(1)} %all-to-all-done) | copy-start | bytes 786436
  52.9 20.0 %all-to-all-start.1 = ((f32[128,2,128]{2,1,0:T(2,128)}), f32[128,2,128]{2,1,0:T(2,128)S(1)}, u32[]{:S(2)}, u32[]{:S(2)}) async-start(f32[128,2,128]{2,1,0:T(2,128)} %bitcast.18), calls=%async_computation.1 | async-start | bytes 262144 | tf_op jit(solution)/shard_map/all_to_all | solution.py:233
  72.9 0.6 copy-start.1
  84.0 14.7 %all-to-all-start.2 = ((f32[128,4,128]{2,1,0:T(4,128)}), f32[128,4,128]{2,1,0:T(4,128)S(1)}, u32[]{:S(2)}, u32[]{:S(2)}) async-start(f32[128,4,128]{2,1,0:T(4,128)} %bitcast.58), calls=%async_computation.2 | async-start | bytes 524288 | tf_op jit(solution)/shard_map/all_to_all | solution.py:233
  99.4 34.6 %all-to-all-start.3 = ((f32[128,2,128]{2,1,0:T(2,128)}), f32[128,2,128]{2,1,0:T(2,128)S(1)}, u32[]{:S(2)}, u32[]{:S(2)}) async-start(f32[128,2,128]{2,1,0:T(2,128)} %bitcast.26), calls=%async_computation.3 | async-start | bytes 262144 | tf_op jit(solution)/shard_map/all_to_all | solution.py:233
  134.0 0.7 copy-start.2
